TPU v7x, 32 devices: a whole 2x2x4 slice. The times are simulated.
32 devices in a mesh: rcv: 32 (over z, y, x, core).
Axes of the slice: x: 2, y: 2, z: 4, core: 2. Of those that a mesh axis runs over, the one named last changes fastest.
Arguments:
- predictions: bfloat16 [32768, 384], P('rcv'), may hold values from -6 to 6
- observed: bfloat16 [2, 32768, 1024], P(None, 'rcv'), may hold values from -0.3984375 to 0.3984375
- partners: int32 [2, 32], replicated, may hold values from 0 to 31, as said below
- green_block: bfloat16 [32768, 512], P('rcv'), may hold values from -0.0625 to 0.0625
Outputs:
- gradient: float32 [512, 384], P('rcv')
Inputs may be any that keep to these rules, and one draw needn't show every extreme that they name: `partners`: row m pairs block b with block b XOR s_m for a meeting offset s_m; s_0 lies in 1 to 30 and s_1 = s_0 XOR (31).
All inputs are finite; a program needn't handle non-finite values.
Results may differ from a plain program's by a relative error of at most 0.0034.
Values may be sent and summed in bfloat16 or wider, within the bound.
No kernel may reach another device: no remote copies, remote signals or barrier semaphores. Data moves between devices by JAX's collectives and lax.ppermute only.
A program may use at most 64 MiB of HBM per device.

v0:
```python
import functools

import jax
import jax.numpy as jnp
from jax import lax
from jax.experimental import pallas as pl
from jax.experimental.pallas import tpu as pltpu
from jax.sharding import PartitionSpec as P

student_nu = 0.01
direct_bits = 5
chunk_rows = 256
turn_rows = 128
f32 = jnp.float32


def send(value, offset):
    if offset == 0:
        return value
    return lax.ppermute(value, "rcv", [(i, i ^ offset) for i in range(lax.axis_size("rcv"))])


def contract_last(left, right):
    return lax.dot_general(left, right, (((1,), (1,)), ((), ())), preferred_element_type=f32)


def turn_kernel(rows_ref, turned_ref):
    turned_ref[...] = rows_ref[...].T


def turn(value):
    rows, samples = value.shape
    return pl.pallas_call(
        turn_kernel,
        out_shape=jax.ShapeDtypeStruct((samples, rows), value.dtype),
        grid=(rows // turn_rows,),
        in_specs=[pl.BlockSpec((turn_rows, samples), lambda c: (c, 0))],
        out_specs=pl.BlockSpec((samples, turn_rows), lambda c: (0, c)),
        compiler_params=pltpu.CompilerParams(dimension_semantics=("arbitrary",)),
    )(value)


def weights_of(gram, tile_obs, samples):
    residual = gram - tile_obs.astype(f32) * samples
    weights = ((student_nu + 1.0) * samples) * residual
    weights = weights / (student_nu * samples * samples + residual * residual)
    return weights.astype(jnp.bfloat16)


def pair_kernel(
    far_steps, _, mine_ref, mine_t, far_ref, near_ref, odd_obs, even_obs,
    far_back, near_back, even_weights, odd_weights, odd_gram, held_weights,
):
    step = pl.program_id(0)
    samples = mine_ref.shape[1]
    rows = jnp.where(step < far_steps, far_ref[...], near_ref[...])
    back_even = jnp.dot(mine_t[...], held_weights[...], preferred_element_type=f32)
    odd = weights_of(odd_gram[...], odd_obs[...], samples)
    even_gram = contract_last(mine_ref[...], rows[:chunk_rows])
    odd_weights[...] = odd
    back_odd = jnp.dot(mine_t[...], odd, preferred_element_type=f32)
    even = weights_of(even_gram, even_obs[...], samples)
    even_weights[...] = even
    held_weights[...] = even
    odd_gram[...] = contract_last(mine_ref[...], rows[chunk_rows:])
    back_even = (back_even * (1.0 / samples)).astype(jnp.bfloat16)
    back_odd = (back_odd * (1.0 / samples)).astype(jnp.bfloat16)

    @pl.when(step <= far_steps)
    def _():
        far_back[:, :chunk_rows] = back_even
        far_back[:, chunk_rows:] = back_odd

    @pl.when(step > far_steps)
    def _():
        near_back[:, :chunk_rows] = back_even
        near_back[:, chunk_rows:] = back_odd


def pair_products(mine, mine_t, far_rows, near_rows, observed, far_index):
    rows, samples = mine.shape
    chunks = rows // chunk_rows
    steps = rows // (2 * chunk_rows)
    double = 2 * chunk_rows

    def rows_at(first):
        return lambda s, far: (jnp.clip(s - first, 0, steps - 1), 0)

    def back_at(first):
        return lambda s, far: (0, jnp.clip(s - first, 0, steps - 1))

    def observed_at(shift):
        def at(s, far):
            chunk = jnp.clip(2 * s + shift, 0, 2 * chunks - 1)
            later = chunk >= chunks
            return jnp.where(later, 1 - far[0], far[0]), 0, jnp.where(later, chunk - chunks, chunk)

        return at

    tile = (None, rows, chunk_rows)
    back = jax.ShapeDtypeStruct((samples, rows), jnp.bfloat16)
    weights = jax.ShapeDtypeStruct((rows, (2 * steps + 1) * chunk_rows), jnp.bfloat16)
    return pl.pallas_call(
        functools.partial(pair_kernel, steps),
        out_shape=(back, back, weights, weights),
        grid_spec=pltpu.PrefetchScalarGridSpec(
            num_scalar_prefetch=1,
            grid=(2 * steps + 1,),
            in_specs=[
                pl.BlockSpec((rows, samples), lambda s, far: (0, 0)),
                pl.BlockSpec((samples, rows), lambda s, far: (0, 0)),
                pl.BlockSpec((double, samples), rows_at(0)),
                pl.BlockSpec((double, samples), rows_at(steps)),
                pl.BlockSpec(tile, observed_at(-1)),
                pl.BlockSpec(tile, observed_at(0)),
            ],
            out_specs=[
                pl.BlockSpec((samples, double), back_at(1)),
                pl.BlockSpec((samples, double), back_at(steps + 1)),
                pl.BlockSpec((rows, chunk_rows), lambda s, far: (0, s)),
                pl.BlockSpec((rows, chunk_rows), lambda s, far: (0, s)),
            ],
            scratch_shapes=[
                pltpu.VMEM((rows, chunk_rows), f32),
                pltpu.VMEM((rows, chunk_rows), jnp.bfloat16),
            ],
        ),
        compiler_params=pltpu.CompilerParams(dimension_semantics=("arbitrary",)),
    )(far_index, mine, mine_t, far_rows, near_rows, observed, observed)


def own_kernel(far_steps, far_ref, near_ref, even_weights, odd_weights, own_ref, total):
    step = pl.program_id(1)
    rows = jnp.where(step < far_steps, far_ref[...], near_ref[...])
    own = jnp.dot(even_weights[...], rows[:chunk_rows], preferred_element_type=f32)
    own += jnp.dot(odd_weights[...], rows[chunk_rows:], preferred_element_type=f32)
    total[...] = jnp.where(step == 0, own, total[...] + own)

    @pl.when(step == pl.num_programs(1) - 1)
    def _():
        own_ref[...] = (total[...] * (1.0 / far_ref.shape[1])).T


def own_product(far, near, even_weights, odd_weights):
    rows, samples = far.shape
    steps = rows // (2 * chunk_rows)
    double = 2 * chunk_rows
    return pl.pallas_call(
        functools.partial(own_kernel, steps),
        out_shape=jax.ShapeDtypeStruct((samples, rows), f32),
        grid=(rows // chunk_rows, 2 * steps),
        in_specs=[
            pl.BlockSpec((double, samples), lambda c, s: (jnp.clip(s, 0, steps - 1), 0)),
            pl.BlockSpec((double, samples), lambda c, s: (jnp.clip(s - steps, 0, steps - 1), 0)),
            pl.BlockSpec((chunk_rows, chunk_rows), lambda c, s: (c, s)),
            pl.BlockSpec((chunk_rows, chunk_rows), lambda c, s: (c, s + 1)),
        ],
        out_specs=pl.BlockSpec((samples, chunk_rows), lambda c, s: (0, c)),
        scratch_shapes=[pltpu.VMEM((chunk_rows, samples), f32)],
        compiler_params=pltpu.CompilerParams(dimension_semantics=("arbitrary", "arbitrary")),
    )(far, near, even_weights, odd_weights)


def partial_kernel(order, here_ref, own_ref, far_ref, near_ref, green_ref, *outs_and_scratch):
    outs, (total, turned) = outs_and_scratch[:-2], outs_and_scratch[-2:]
    chunk = pl.program_id(0)
    adjoint = own_ref[...] + far_ref[...].astype(f32) + near_ref[...].astype(f32)
    product = jnp.dot(adjoint.astype(jnp.bfloat16), green_ref[...], preferred_element_type=f32)

    @pl.when(chunk == 0)
    def _():
        total[...] = product

    @pl.when(chunk > 0)
    def _():
        total[...] += product

    @pl.when(chunk == pl.num_programs(0) - 1)
    def _():
        turned[...] = total[...].T
        block = turned.shape[0] // len(order)
        each = len(order) // len(outs)
        for place, index in enumerate(order):
            source = pl.multiple_of((here_ref[0] ^ index) * block, block)
            spot = place % each * block
            outs[place // each][spot : spot + block, :] = turned[pl.ds(source, block), :]


def partial_gradient(here, own, far_return, near_return, green_block, order, parts):
    samples, rows = own.shape
    cells = green_block.shape[1]
    natural = cells // len(order) % 8 != 0
    kernel_order, kernel_parts = ([0], 1) if natural else (order, parts)
    column = pl.BlockSpec((samples, chunk_rows), lambda c, here: (0, c))
    size = cells // kernel_parts
    outs = pl.pallas_call(
        functools.partial(partial_kernel, kernel_order),
        out_shape=[jax.ShapeDtypeStruct((size, samples), f32)] * kernel_parts,
        grid_spec=pltpu.PrefetchScalarGridSpec(
            num_scalar_prefetch=1,
            grid=(rows // chunk_rows,),
            in_specs=[column] * 3 + [pl.BlockSpec((chunk_rows, cells), lambda c, here: (c, 0))],
            out_specs=[pl.BlockSpec((size, samples), lambda c, here: (0, 0))] * kernel_parts,
            scratch_shapes=[pltpu.VMEM((samples, cells), f32), pltpu.VMEM((cells, samples), f32)],
        ),
        compiler_params=pltpu.CompilerParams(dimension_semantics=("arbitrary",)),
    )(here * 0 if natural else here, own, far_return, near_return, green_block)
    if natural:
        blocks = outs[0].reshape(len(order), cells // len(order), samples)
        wanted = jnp.bitwise_xor(jnp.array(order, jnp.int32), here)
        blocks = jnp.take(blocks, wanted, axis=0).reshape(parts, cells // parts, samples)
        outs = [blocks[part] for part in range(parts)]
    return list(outs)


def route_high(near, far, near_offset, low_bits, count_bits):
    for level in range(low_bits, count_bits):
        takes_near = near_offset >> level & 1 == 1
        moved = send(jnp.where(takes_near, near, far), 1 << level)
        near = jnp.where(takes_near, moved, near)
        far = jnp.where(takes_near, far, moved)
    return near, far


def meet_both(near, far, mine, observed, near_offset, far_index, low_bits, count_bits):
    mask = (1 << low_bits) - 1
    lowest = 1 if low_bits == count_bits else 0
    offsets = range(lowest, 1 << low_bits - 1)

    def arrive(offset):
        def run(near, far, mine):
            far_rows = send(far, offset ^ mask)
            return far_rows, send(near, offset), turn(mine)

        return run

    def leave(offset):
        def run(far_rows, near_rows, far_back, near_back, *weights):
            far_return = send(far_back, offset ^ mask)
            near_return = send(near_back, offset)
            return own_product(far_rows, near_rows, *weights), far_return, near_return

        return run

    chosen = (near_offset & mask) - lowest
    far_rows, near_rows, mine_t = lax.switch(
        chosen, [arrive(offset) for offset in offsets], near, far, mine
    )
    products = pair_products(mine, mine_t, far_rows, near_rows, observed, far_index)
    return lax.switch(
        chosen, [leave(offset) for offset in offsets], far_rows, near_rows, *products
    )


def stage_groups(count_bits):
    groups, level = [], 0
    while level < count_bits:
        width = min(1 if level == 0 else 2, count_bits - level)
        groups.append((level, width))
        level += width
    return groups


def xor_order(groups):
    order = [0]
    for level, width in groups:
        order = [block | digit << level for block in order for digit in range(1 << width)]
    return order


def scatter_sum(parts, groups):
    total = None
    for level, width in groups:
        if total is not None:
            size = total.shape[0] >> width
            parts = [total[digit * size : (digit + 1) * size] for digit in range(1 << width)]
        moved = [send(parts[digit], digit << level) for digit in range(1, 1 << width)]
        total = parts[0]
        for piece in moved:
            total = total + piece
    return total


def shards(predictions, observed, partners, green_block):
    count_bits = lax.axis_size("rcv").bit_length() - 1
    low_bits = min(direct_bits, count_bits)
    here = lax.axis_index("rcv").astype(jnp.int32).reshape(1)
    first_offset = partners[0, 0]
    first_far = first_offset >> low_bits - 1 & 1
    near_offset = jnp.where(first_far == 1, partners[1, 0], first_offset)
    far_index = (1 - first_far).reshape(1)

    near_in, far_in = route_high(predictions, predictions, near_offset, low_bits, count_bits)
    own, far_return, near_return = meet_both(
        near_in, far_in, predictions, observed, near_offset, far_index, low_bits, count_bits
    )
    near_return, far_return = route_high(near_return, far_return, near_offset, low_bits, count_bits)

    groups = stage_groups(count_bits)
    parts = partial_gradient(
        here, own, far_return, near_return, green_block, xor_order(groups), 1 << groups[0][1]
    )
    return scatter_sum(parts, groups)


def solution(mesh):
    placed = (P("rcv", None), P(None, "rcv", None), P(), P("rcv", None))
    return jax.shard_map(
        shards, mesh=mesh, in_specs=placed, out_specs=P("rcv", None), check_vma=False
    )
```

profile of v0, /device:TPU:0, one launch (start us, length us, event | category | flops | bytes accessed | tf_op | source)
XLA Modules:
  0.0 103.5 jit_solution(9675670706989838075)
XLA Ops:
  0.0 1.3 %fusion.6 = (s32[1,1]{1,0:T(1,128)}, s32[1,1]{1,0:T(1,128)}) fusion(s32[2,32]{1,0:T(2,128)} %param.36), kind=kLoop, calls=%fused_computation.8 | loop fusion | bytes 16 | tf_op jit(solution)/shard_map/slice | solution.py:290
  3.2 26.0 %conditional.2 = (bf16[1024,384]{1,0:T(8,128)(2,1)}, bf16[1024,384]{1,0:T(8,128)(2,1)}, bf16[384,1024]{1,0:T(8,128)(2,1)S(1)}) conditional(s32[]{:T(128)} %clamp.4, bf16[1024,384]{1,0:T(8,128)(2,1)} %mine_ref.1, bf16[1024,384]{1,0:T(8,128)(2,1)} %mine_ref.1, bf16[1024,384]{1,0:T(8,128)(2,1)} %mine_ref.1, ...), branch_computations={%region_0.1_spmd, %region_1.2_spmd, %region_2.3_spmd, %region_3.4_... | conditional | bytes 6291560 | solution.py:246
  3.3 5.5 %collective-permute-start.2 = (bf16[1024,384]{1,0:T(8,128)(2,1)}, bf16[1024,384]{1,0:T(8,128)(2,1)}, u32[]{:S(2)}, u32[]{:S(2)}) collective-permute-start(bf16[1024,384]{1,0:T(8,128)(2,1)} %rows_ref.1), channel_id=1, source_target_pairs={{0,29},{1,28},{2,31},{3,30},{4,25},{5,24},{6,27},{7,26},{8,21},{9,... | collective-permute-start | bytes 2359304 | tf_op jit(solution)/shard_map/cond/branch_1_fun/ppermute | solution.py:20
  8.8 1.5 %collective-permute-start.3 = (bf16[1024,384]{1,0:T(8,128)(2,1)}, bf16[1024,384]{1,0:T(8,128)(2,1)}, u32[]{:S(2)}, u32[]{:S(2)}) collective-permute-start(bf16[1024,384]{1,0:T(8,128)(2,1)} %rows_ref.1), channel_id=1, source_target_pairs={{0,2},{1,3},{2,0},{3,1},{4,6},{5,7},{6,4},{7,5},{8,10},{9,11},{10,... | collective-permute-start | bytes 2359304 | tf_op jit(solution)/shard_map/cond/branch_1_fun/ppermute | solution.py:20
  10.3 4.2 %branch_1_fun.2 = bf16[384,1024]{1,0:T(8,128)(2,1)S(1)} custom-call(bf16[1024,384]{1,0:T(8,128)(2,1)} %rows_ref.1), custom_call_target="tpu_custom_call" | custom-call | tf_op jit(solution)/shard_map/cond/branch_1_fun/pallas_call | solution.py:33
  14.5 12.6 %collective-permute-done.2 = bf16[1024,384]{1,0:T(8,128)(2,1)} collective-permute-done((bf16[1024,384]{1,0:T(8,128)(2,1)}, bf16[1024,384]{1,0:T(8,128)(2,1)}, u32[]{:S(2)}, u32[]{:S(2)}) %collective-permute-start.2) | collective-permute-done | bytes 786464 | tf_op jit(solution)/shard_map/cond/branch_1_fun/ppermute | solution.py:20
  27.1 2.2 %collective-permute-done.3 = bf16[1024,384]{1,0:T(8,128)(2,1)} collective-permute-done((bf16[1024,384]{1,0:T(8,128)(2,1)}, bf16[1024,384]{1,0:T(8,128)(2,1)}, u32[]{:S(2)}, u32[]{:S(2)}) %collective-permute-start.3) | collective-permute-done | bytes 786464 | tf_op jit(solution)/shard_map/cond/branch_1_fun/ppermute | solution.py:20
  29.2 10.5 %shard_map.91 = (bf16[384,1024]{1,0:T(8,128)(2,1)}, bf16[384,1024]{1,0:T(8,128)(2,1)}, bf16[1024,1280]{1,0:T(8,128)(2,1)S(1)}, bf16[1024,1280]{1,0:T(8,128)(2,1)}) custom-call(s32[1]{0:T(128)} %bitcast.3._, bf16[1024,384]{1,0:T(8,128)(2,1)} %mine_ref.1, bf16[384,1024]{1,0:T(8,128)(2,1)S(1)} %get-tuple-element.304.mine_t, ...), custom_call_target="tpu_custom_call" | custom-call | tf_op jit(solution)/shard_map/pallas_call | solution.py:103
  39.7 23.0 %conditional.3 = (f32[384,1024]{1,0:T(8,128)}, bf16[384,1024]{1,0:T(8,128)(2,1)}, bf16[384,1024]{1,0:T(8,128)(2,1)}) conditional(s32[]{:T(128)} %clamp.4, (bf16[1024,384]{1,0:T(8,128)(2,1)}, bf16[1024,384]{1,0:T(8,128)(2,1)}, bf16[1024,1280]{1,0:T(8,128)(2,1)S(1)}, bf16[1024,1280]{1,0:T(8,128)(2,1)}, ...), branch_computations={%region_15.16_spmd, %region_16.17_spmd, %region_17.18_spmd, %regio... | conditional | bytes 6291560 | solution.py:250
  39.7 2.8 %collective-permute-start.32 = (bf16[384,1024]{1,0:T(8,128)(2,1)}, bf16[384,1024]{1,0:T(8,128)(2,1)}, u32[]{:S(2)}, u32[]{:S(2)}) collective-permute-start(bf16[384,1024]{1,0:T(8,128)(2,1)} %get-tuple-element.210), channel_id=1, source_target_pairs={{0,29},{1,28},{2,31},{3,30},{4,25},{5,24},{6,27},{7,26},{8,21},{9,... | collective-permute-start | bytes 2359304 | tf_op jit(solution)/shard_map/cond/branch_1_fun/ppermute | solution.py:20
  42.5 1.5 %collective-permute-start.33 = (bf16[384,1024]{1,0:T(8,128)(2,1)}, bf16[384,1024]{1,0:T(8,128)(2,1)}, u32[]{:S(2)}, u32[]{:S(2)}) collective-permute-start(bf16[384,1024]{1,0:T(8,128)(2,1)} %get-tuple-element.211), channel_id=1, source_target_pairs={{0,2},{1,3},{2,0},{3,1},{4,6},{5,7},{6,4},{7,5},{8,10},{9,11},{10,... | collective-permute-start | bytes 2359304 | tf_op jit(solution)/shard_map/cond/branch_1_fun/ppermute | solution.py:20
  44.0 13.4 %branch_1_fun.3 = f32[384,1024]{1,0:T(8,128)} custom-call(bf16[1024,384]{1,0:T(8,128)(2,1)} %get-tuple-element.206.far_ref, bf16[1024,384]{1,0:T(8,128)(2,1)} %get-tuple-element.207.near_ref, bf16[1024,1280]{1,0:T(8,128)(2,1)S(1)} %get-tuple-element.208.even_weights, bf16[1024,1280]{1,0:T(8,128)(2,1)} %get-tuple-element.209.odd_weights), custom_call_target="tpu_custom_call" | custom-call | tf_op jit(solution)/shard_map/cond/branch_1_fun/pallas_call | solution.py:148
  57.4 5.3 %collective-permute-done.32 = bf16[384,1024]{1,0:T(8,128)(2,1)} collective-permute-done((bf16[384,1024]{1,0:T(8,128)(2,1)}, bf16[384,1024]{1,0:T(8,128)(2,1)}, u32[]{:S(2)}, u32[]{:S(2)}) %collective-permute-start.32) | collective-permute-done | bytes 786464 | tf_op jit(solution)/shard_map/cond/branch_1_fun/ppermute | solution.py:20
  62.7 4.8 %shard_map.92 = (f32[256,384]{1,0:T(8,128)}, f32[256,384]{1,0:T(8,128)}) custom-call(s32[1]{0:T(128)} %bitcast.here_ref, f32[384,1024]{1,0:T(8,128)} %get-tuple-element.309.own_ref, bf16[384,1024]{1,0:T(8,128)(2,1)} %get-tuple-element.310.far_ref, bf16[384,1024]{1,0:T(8,128)(2,1)} %get-tuple-element.311.near_ref, bf16[1024,512]{1,0:T(8,128)(2,1)} %green_ref.1), custom_call_target="tpu_custom_call" | custom-call | tf_op jit(solution)/shard_map/pallas_call | solution.py:196
  67.5 1.9 %collective-permute-done.60 = f32[256,384]{1,0:T(8,128)S(1)} collective-permute-done((f32[256,384]{1,0:T(8,128)}, f32[256,384]{1,0:T(8,128)S(1)}, u32[]{:S(2)}, u32[]{:S(2)}) %collective-permute-start.60) | collective-permute-done | bytes 393248 | tf_op jit(solution)/shard_map/ppermute | solution.py:20
  70.5 1.6 %collective-permute-start.61 = (f32[64,384]{1,0:T(8,128)S(1)}, f32[64,384]{1,0:T(8,128)S(1)}, u32[]{:S(2)}, u32[]{:S(2)}) collective-permute-start(f32[64,384]{1,0:T(8,128)S(1)} %get-tuple-element.314), channel_id=1, source_target_pairs={{0,2},{1,3},{2,0},{3,1},{4,6},{5,7},{6,4},{7,5},{8,10},{9,11},{10,... | collective-permute-start | bytes 294920 | tf_op jit(solution)/shard_map/ppermute | solution.py:20
  72.6 1.5 %collective-permute-start.63 = (f32[64,384]{1,0:T(8,128)S(1)}, f32[64,384]{1,0:T(8,128)S(1)}, u32[]{:S(2)}, u32[]{:S(2)}) collective-permute-start(f32[64,384]{1,0:T(8,128)S(1)} %get-tuple-element.315), channel_id=1, source_target_pairs={{0,6},{1,7},{2,4},{3,5},{4,2},{5,3},{6,0},{7,1},{8,14},{9,15},{10,... | collective-permute-start | bytes 294920 | tf_op jit(solution)/shard_map/ppermute | solution.py:20
  74.1 1.3 %collective-permute-done.61 = f32[64,384]{1,0:T(8,128)S(1)} collective-permute-done((f32[64,384]{1,0:T(8,128)S(1)}, f32[64,384]{1,0:T(8,128)S(1)}, u32[]{:S(2)}, u32[]{:S(2)}) %collective-permute-start.61) | collective-permute-done | bytes 98336 | tf_op jit(solution)/shard_map/ppermute | solution.py:20
  75.4 3.4 %collective-permute-done.62 = f32[64,384]{1,0:T(8,128)S(1)} collective-permute-done((f32[64,384]{1,0:T(8,128)S(1)}, f32[64,384]{1,0:T(8,128)S(1)}, u32[]{:S(2)}, u32[]{:S(2)}) %collective-permute-start.62) | collective-permute-done | bytes 98336 | tf_op jit(solution)/shard_map/ppermute | solution.py:20
  78.8 17.3 %collective-permute-start.64 = (f32[16,384]{1,0:T(8,128)S(1)}, f32[16,384]{1,0:T(8,128)S(1)}, u32[]{:S(2)}, u32[]{:S(2)}) collective-permute-start(f32[16,384]{1,0:T(8,128)S(1)} %get-tuple-element.317), channel_id=1, source_target_pairs={{0,8},{1,9},{2,10},{3,11},{4,12},{5,13},{6,14},{7,15},{8,0},{9,1},... | collective-permute-start | bytes 73736 | tf_op jit(solution)/shard_map/ppermute | solution.py:20
  96.2 1.1 %collective-permute-start.65 = (f32[16,384]{1,0:T(8,128)S(1)}, f32[16,384]{1,0:T(8,128)S(1)}, u32[]{:S(2)}, u32[]{:S(2)}) collective-permute-start(f32[16,384]{1,0:T(8,128)S(1)} %get-tuple-element.319), channel_id=1, source_target_pairs={{0,16},{1,17},{2,18},{3,19},{4,20},{5,21},{6,22},{7,23},{8,24},{9,... | collective-permute-start | bytes 73736 | tf_op jit(solution)/shard_map/ppermute | solution.py:20
  97.2 1.4 %collective-permute-start.66 = (f32[16,384]{1,0:T(8,128)S(1)}, f32[16,384]{1,0:T(8,128)S(1)}, u32[]{:S(2)}, u32[]{:S(2)}) collective-permute-start(f32[16,384]{1,0:T(8,128)S(1)} %get-tuple-element.318), channel_id=1, source_target_pairs={{0,24},{1,25},{2,26},{3,27},{4,28},{5,29},{6,30},{7,31},{8,16},{9,... | collective-permute-start | bytes 73736 | tf_op jit(solution)/shard_map/ppermute | solution.py:20
  98.6 2.3 %collective-permute-done.65 = f32[16,384]{1,0:T(8,128)S(1)} collective-permute-done((f32[16,384]{1,0:T(8,128)S(1)}, f32[16,384]{1,0:T(8,128)S(1)}, u32[]{:S(2)}, u32[]{:S(2)}) %collective-permute-start.65) | collective-permute-done | bytes 24608 | tf_op jit(solution)/shard_map/ppermute | solution.py:20
  101.0 1.9 %collective-permute-done.66 = f32[16,384]{1,0:T(8,128)S(1)} collective-permute-done((f32[16,384]{1,0:T(8,128)S(1)}, f32[16,384]{1,0:T(8,128)S(1)}, u32[]{:S(2)}, u32[]{:S(2)}) %collective-permute-start.66) | collective-permute-done | bytes 24608 | tf_op jit(solution)/shard_map/ppermute | solution.py:20
  (10 shorter events, 2.3 us)
Async XLA Ops:
  3.3 23.8 %collective-permute-start.2 = (bf16[1024,384]{1,0:T(8,128)(2,1)}, bf16[1024,384]{1,0:T(8,128)(2,1)}, u32[]{:S(2)}, u32[]{:S(2)}) collective-permute-start(bf16[1024,384]{1,0:T(8,128)(2,1)} %rows_ref.1), channel_id=1, source_target_pairs={{0,29},{1,28},{2,31},{3,30},{4,25},{5,24},{6,27},{7,26},{8,21},{9,... | collective-permute-start | bytes 2359304 | tf_op jit(solution)/shard_map/cond/branch_1_fun/ppermute | solution.py:20
  8.8 20.4 %collective-permute-start.3 = (bf16[1024,384]{1,0:T(8,128)(2,1)}, bf16[1024,384]{1,0:T(8,128)(2,1)}, u32[]{:S(2)}, u32[]{:S(2)}) collective-permute-start(bf16[1024,384]{1,0:T(8,128)(2,1)} %rows_ref.1), channel_id=1, source_target_pairs={{0,2},{1,3},{2,0},{3,1},{4,6},{5,7},{6,4},{7,5},{8,10},{9,11},{10,... | collective-permute-start | bytes 2359304 | tf_op jit(solution)/shard_map/cond/branch_1_fun/ppermute | solution.py:20
  39.7 23.0 %collective-permute-start.32 = (bf16[384,1024]{1,0:T(8,128)(2,1)}, bf16[384,1024]{1,0:T(8,128)(2,1)}, u32[]{:S(2)}, u32[]{:S(2)}) collective-permute-start(bf16[384,1024]{1,0:T(8,128)(2,1)} %get-tuple-element.210), channel_id=1, source_target_pairs={{0,29},{1,28},{2,31},{3,30},{4,25},{5,24},{6,27},{7,26},{8,21},{9,... | collective-permute-start | bytes 2359304 | tf_op jit(solution)/shard_map/cond/branch_1_fun/ppermute | solution.py:20
  42.5 20.2 %collective-permute-start.33 = (bf16[384,1024]{1,0:T(8,128)(2,1)}, bf16[384,1024]{1,0:T(8,128)(2,1)}, u32[]{:S(2)}, u32[]{:S(2)}) collective-permute-start(bf16[384,1024]{1,0:T(8,128)(2,1)} %get-tuple-element.211), channel_id=1, source_target_pairs={{0,2},{1,3},{2,0},{3,1},{4,6},{5,7},{6,4},{7,5},{8,10},{9,11},{10,... | collective-permute-start | bytes 2359304 | tf_op jit(solution)/shard_map/cond/branch_1_fun/ppermute | solution.py:20
  67.5 1.9 %collective-permute-start.60 = (f32[256,384]{1,0:T(8,128)}, f32[256,384]{1,0:T(8,128)S(1)}, u32[]{:S(2)}, u32[]{:S(2)}) collective-permute-start(f32[256,384]{1,0:T(8,128)} %get-tuple-element.313), channel_id=1, source_target_pairs={{0,1},{1,0},{2,3},{3,2},{4,5},{5,4},{6,7},{7,6},{8,9},{9,8},{10,11... | collective-permute-start | bytes 1179656 | tf_op jit(solution)/shard_map/ppermute | solution.py:20
  70.5 4.9 %collective-permute-start.61 = (f32[64,384]{1,0:T(8,128)S(1)}, f32[64,384]{1,0:T(8,128)S(1)}, u32[]{:S(2)}, u32[]{:S(2)}) collective-permute-start(f32[64,384]{1,0:T(8,128)S(1)} %get-tuple-element.314), channel_id=1, source_target_pairs={{0,2},{1,3},{2,0},{3,1},{4,6},{5,7},{6,4},{7,5},{8,10},{9,11},{10,... | collective-permute-start | bytes 294920 | tf_op jit(solution)/shard_map/ppermute | solution.py:20
  72.1 6.7 %collective-permute-start.62 = (f32[64,384]{1,0:T(8,128)S(1)}, f32[64,384]{1,0:T(8,128)S(1)}, u32[]{:S(2)}, u32[]{:S(2)}) collective-permute-start(f32[64,384]{1,0:T(8,128)S(1)} %get-tuple-element.316), channel_id=1, source_target_pairs={{0,4},{1,5},{2,6},{3,7},{4,0},{5,1},{6,2},{7,3},{8,12},{9,13},{10,... | collective-permute-start | bytes 294920 | tf_op jit(solution)/shard_map/ppermute | solution.py:20
  72.6 6.2 %collective-permute-start.63 = (f32[64,384]{1,0:T(8,128)S(1)}, f32[64,384]{1,0:T(8,128)S(1)}, u32[]{:S(2)}, u32[]{:S(2)}) collective-permute-start(f32[64,384]{1,0:T(8,128)S(1)} %get-tuple-element.315), channel_id=1, source_target_pairs={{0,6},{1,7},{2,4},{3,5},{4,2},{5,3},{6,0},{7,1},{8,14},{9,15},{10,... | collective-permute-start | bytes 294920 | tf_op jit(solution)/shard_map/ppermute | solution.py:20
  78.8 19.8 %collective-permute-start.64 = (f32[16,384]{1,0:T(8,128)S(1)}, f32[16,384]{1,0:T(8,128)S(1)}, u32[]{:S(2)}, u32[]{:S(2)}) collective-permute-start(f32[16,384]{1,0:T(8,128)S(1)} %get-tuple-element.317), channel_id=1, source_target_pairs={{0,8},{1,9},{2,10},{3,11},{4,12},{5,13},{6,14},{7,15},{8,0},{9,1},... | collective-permute-start | bytes 73736 | tf_op jit(solution)/shard_map/ppermute | solution.py:20
  96.2 4.8 %collective-permute-start.65 = (f32[16,384]{1,0:T(8,128)S(1)}, f32[16,384]{1,0:T(8,128)S(1)}, u32[]{:S(2)}, u32[]{:S(2)}) collective-permute-start(f32[16,384]{1,0:T(8,128)S(1)} %get-tuple-element.319), channel_id=1, source_target_pairs={{0,16},{1,17},{2,18},{3,19},{4,20},{5,21},{6,22},{7,23},{8,24},{9,... | collective-permute-start | bytes 73736 | tf_op jit(solution)/shard_map/ppermute | solution.py:20
  97.2 5.6 %collective-permute-start.66 = (f32[16,384]{1,0:T(8,128)S(1)}, f32[16,384]{1,0:T(8,128)S(1)}, u32[]{:S(2)}, u32[]{:S(2)}) collective-permute-start(f32[16,384]{1,0:T(8,128)S(1)} %get-tuple-element.318), channel_id=1, source_target_pairs={{0,24},{1,25},{2,26},{3,27},{4,28},{5,29},{6,30},{7,31},{8,16},{9,... | collective-permute-start | bytes 73736 | tf_op jit(solution)/shard_map/ppermute | solution.py:20
where the time goes:
time: 103 us
  starting transfers between devices  34.7 us (34%)
  Pallas kernels  32.9 us (32%)
  waiting for transfers between devices  30.9 us (30%)
  between operations  1.96 us (2%)
  other arithmetic  1.68 us (2%)
  local copies, waits for them, and re-layouts  1.32 us (1%)
    ppermute x11, starting transfers between devices, send(): lax.ppermute(value, 'rcv', [(i, i ^ offset) for i in range(lax.axis_size(...  34.7 us
    ppermute x11, waiting for transfers between devices, send(): lax.ppermute(value, 'rcv', [(i, i ^ offset) for i in range(lax.axis_size(...  30.9 us
    pallas_call x1, Pallas kernels, own_product(): pl.pallas_call(functools.partial(own_kernel, steps), out_shape=jax.ShapeD...  13.4 us
    pallas_call x1, Pallas kernels, pair_products(): pl.pallas_call(functools.partial(pair_kernel, steps), out_shape=(back, ba...  10.5 us
    pallas_call x1, Pallas kernels, partial_gradient(): pl.pallas_call(functools.partial(partial_kernel, kernel_order), out_shape...  4.81 us
    pallas_call x1, Pallas kernels, turn(): pl.pallas_call(turn_kernel, out_shape=jax.ShapeDtypeStruct((samples, rows...  4.19 us
  transfers between devices with their start and end apart: 11, of which 8 were waited for; matrix products, arithmetic and copies ran while one was open for 0% of the time, Pallas kernels for 17%

commit v1 on v0

--- a/solution.py
+++ b/solution.py
@@ -10,6 +10,7 @@
 student_nu = 0.01
 direct_bits = 5
 chunk_rows = 256
+block_rows = 1024
 turn_rows = 128
 f32 = jnp.float32
 
@@ -18,6 +19,18 @@
     if offset == 0:
         return value
     return lax.ppermute(value, "rcv", [(i, i ^ offset) for i in range(lax.axis_size("rcv"))])
+
+
+def is_mixed(device, top):
+    return (device >> top ^ device >> top - 1) & 1 == 1
+
+
+def send_mixed(value, mixed_offset, other_offset, top):
+    pairs = [
+        (i, i ^ (mixed_offset if is_mixed(i, top) else other_offset))
+        for i in range(lax.axis_size("rcv"))
+    ]
+    return lax.ppermute(value, "rcv", pairs)
 
 
 def contract_last(left, right):
@@ -222,10 +235,84 @@
     return near, far
 
 
-def meet_both(near, far, mine, observed, near_offset, far_index, low_bits, count_bits):
+def back_kernel(_, mine_ref, mine_t, other_ref, obs_ref, back_ref, weights_ref, *scratch):
+    block, last = pl.program_id(1), pl.num_programs(1) - 1
+    samples = mine_ref.shape[1]
+    gram = contract_last(mine_ref[...], other_ref[...])
+    weights = weights_of(gram, obs_ref[...], samples)
+    weights_ref[...] = weights
+    back = jnp.dot(mine_t[...], weights, preferred_element_type=f32)
+    if not scratch:
+        back_ref[...] = (back * (1.0 / samples)).astype(jnp.bfloat16)
+        return
+    (total,) = scratch
+    back = jnp.where(block == 0, back, total[...] + back)
+    total[...] = back
+
+    @pl.when(block == last)
+    def _():
+        back_ref[...] = (back * (1.0 / samples)).astype(jnp.bfloat16)
+
+
+def back_product(mine, mine_t, other, observed, meeting):
+    rows, samples = mine.shape
+    blocks = rows // block_rows
+    return pl.pallas_call(
+        back_kernel,
+        out_shape=(
+            jax.ShapeDtypeStruct((samples, rows), jnp.bfloat16),
+            jax.ShapeDtypeStruct((rows, rows), jnp.bfloat16),
+        ),
+        grid_spec=pltpu.PrefetchScalarGridSpec(
+            num_scalar_prefetch=1,
+            grid=(rows // chunk_rows, blocks),
+            in_specs=[
+                pl.BlockSpec((block_rows, samples), lambda c, r, meeting: (r, 0)),
+                pl.BlockSpec((samples, block_rows), lambda c, r, meeting: (0, r)),
+                pl.BlockSpec((chunk_rows, samples), lambda c, r, meeting: (c, 0)),
+                pl.BlockSpec(
+                    (None, block_rows, chunk_rows), lambda c, r, meeting: (meeting[0], r, c)
+                ),
+            ],
+            out_specs=[
+                pl.BlockSpec((samples, chunk_rows), lambda c, r, meeting: (0, c)),
+                pl.BlockSpec((block_rows, chunk_rows), lambda c, r, meeting: (r, c)),
+            ],
+            scratch_shapes=[pltpu.VMEM((samples, chunk_rows), f32)] if blocks > 1 else [],
+        ),
+        compiler_params=pltpu.CompilerParams(dimension_semantics=("arbitrary", "arbitrary")),
+    )(meeting, mine, mine_t, other, observed)
+
+
+def total_kernel(first_ref, second_ref, first_weights, second_weights, own_ref, total):
+    step = pl.program_id(1)
+    own = jnp.dot(first_weights[...], first_ref[...], preferred_element_type=f32)
+    own += jnp.dot(second_weights[...], second_ref[...], preferred_element_type=f32)
+    total[...] = jnp.where(step == 0, own, total[...] + own)
+
+    @pl.when(step == pl.num_programs(1) - 1)
+    def _():
+        own_ref[...] = (total[...] * (1.0 / first_ref.shape[1])).T
+
+
+def own_total(first, second, first_weights, second_weights):
+    rows, samples = first.shape
+    values = pl.BlockSpec((chunk_rows, samples), lambda c, s: (s, 0))
+    weights = pl.BlockSpec((chunk_rows, chunk_rows), lambda c, s: (c, s))
+    return pl.pallas_call(
+        total_kernel,
+        out_shape=jax.ShapeDtypeStruct((samples, rows), f32),
+        grid=(rows // chunk_rows, rows // chunk_rows),
+        in_specs=[values, values, weights, weights],
+        out_specs=pl.BlockSpec((samples, chunk_rows), lambda c, s: (0, c)),
+        scratch_shapes=[pltpu.VMEM((chunk_rows, samples), f32)],
+        compiler_params=pltpu.CompilerParams(dimension_semantics=("arbitrary", "arbitrary")),
+    )(first, second, first_weights, second_weights)
+
+
+def meet_apart(near, far, mine, observed, far_index, low_offset, low_bits, lowest):
     mask = (1 << low_bits) - 1
-    lowest = 1 if low_bits == count_bits else 0
-    offsets = range(lowest, 1 << low_bits - 1)
+    offsets = range(lowest, 1 << low_bits - 2)
 
     def arrive(offset):
         def run(near, far, mine):
@@ -242,13 +329,75 @@
 
         return run
 
-    chosen = (near_offset & mask) - lowest
+    chosen = low_offset - lowest
     far_rows, near_rows, mine_t = lax.switch(
         chosen, [arrive(offset) for offset in offsets], near, far, mine
     )
     products = pair_products(mine, mine_t, far_rows, near_rows, observed, far_index)
     return lax.switch(
         chosen, [leave(offset) for offset in offsets], far_rows, near_rows, *products
+    )
+
+
+def meet_mixed(near, far, mine, observed, far_index, low_offset, low_bits):
+    mask = (1 << low_bits) - 1
+    top = low_bits - 1
+    lowest = 1 << top - 1
+    mixed = is_mixed(lax.axis_index("rcv"), top)
+
+    def branch(offset):
+        close, apart = offset, offset ^ mask
+
+        def run(near, far, mine, observed, first_meeting):
+            first_out = near if near is far else jnp.where(mixed, near, far)
+            second_out = near if near is far else jnp.where(mixed, far, near)
+            first = send_mixed(first_out, close, apart, top)
+            second = send_mixed(second_out, apart, close, top)
+            mine_t = turn(mine)
+            back, first_weights = back_product(mine, mine_t, first, observed, first_meeting)
+            first_return = send_mixed(back, apart, close, top)
+            back, second_weights = back_product(mine, mine_t, second, observed, 1 - first_meeting)
+            second_return = send_mixed(back, close, apart, top)
+            own = own_total(first, second, first_weights, second_weights)
+            return own, first_return, second_return
+
+        return run
+
+    first_meeting = jnp.where(mixed, far_index, 1 - far_index)
+    if near is far:
+        one = lambda run: lambda rows, *rest: run(rows, rows, *rest)
+        branches = [one(branch(offset)) for offset in range(lowest, 1 << top)]
+        return lax.switch(low_offset - lowest, branches, near, mine, observed, first_meeting)
+    branches = [branch(offset) for offset in range(lowest, 1 << top)]
+    own, first_return, second_return = lax.switch(
+        low_offset - lowest, branches, near, far, mine, observed, first_meeting
+    )
+    return (
+        own,
+        jnp.where(mixed, second_return, first_return),
+        jnp.where(mixed, first_return, second_return),
+    )
+
+
+def meet_both(near, far, mine, observed, near_offset, far_index, low_bits, count_bits):
+    low_offset = near_offset & (1 << low_bits) - 1
+    lowest = 1 if low_bits == count_bits else 0
+
+    def with_inputs(meet, *more):
+        if near is far:
+            return lambda rows, *rest: meet(rows, rows, *rest, *more)
+        return lambda near, far, *rest: meet(near, far, *rest, *more)
+
+    inputs = (near,) if near is far else (near, far)
+    return lax.cond(
+        low_offset >> low_bits - 2 & 1 == 1,
+        with_inputs(meet_mixed, low_bits),
+        with_inputs(meet_apart, low_bits, lowest),
+        *inputs,
+        mine,
+        observed,
+        far_index,
+        low_offset,
     )
 
 

time: 103 us -> 142 us (1.38); the launches traced: 103 us -> 141 us
  waiting for transfers between devices: 30.9 us -> 49.4 us
  loops' own time: 0.05 us -> 7.41 us
  starting transfers between devices: 34.7 us -> 40.1 us
  Pallas kernels: 32.9 us -> 36.1 us
  local copies, waits for them, and re-layouts: 1.32 us -> 4.3 us
    ppermute x0 -> x4, waiting for transfers between devices: none -> 39 us  [send_mixed(): return lax.ppermute(value, 'rcv', pairs)]
    ppermute x0 -> x4, starting transfers between devices: none -> 32 us  [send_mixed(): return lax.ppermute(value, 'rcv', pairs)]
    ppermute x11 -> x7, starting transfers between devices: 34.7 us -> 8.11 us  [send(): lax.ppermute(value, 'rcv', [(i, i ^ offset) for i in range(lax.axis_size(...]
    ppermute x11 -> x7, waiting for transfers between devices: 30.9 us -> 10.4 us  [send(): lax.ppermute(value, 'rcv', [(i, i ^ offset) for i in range(lax.axis_size(...]
    another operation x2, loops' own time: 0.05 us -> 7.41 us  [the longest x1 7.37 us: meet_mixed(): lax.switch(low_offset - lowest, branches, near, mine, observed, first_mee...]
    cond x0 -> x8, local copies, waits for them, and re-layouts: none -> 2.94 us
    pallas_call x2 -> x3, Pallas kernels: 23.9 us -> 26 us  [the longest x2 13.2 us: back_product(): pl.pallas_call(back_kernel, out_shape=(jax.ShapeDtypeStruct((samples, row...]
  transfers between devices with their start and end apart: 11 -> 11, of which waited for: 8 -> 9; matrix products, arithmetic and copies ran while one was open for 0% -> 0% of each run, Pallas kernels for 17% -> 22%
where the time goes in v1:
time: 142 us; the launch traced here: 141 us
  waiting for transfers between devices  49.4 us (35%)
  starting transfers between devices  40.1 us (28%)
  Pallas kernels  36.1 us (25%)
  loops' own time  7.41 us (5%)
  local copies, waits for them, and re-layouts  4.3 us (3%)
  between operations  1.95 us (1%)
  other arithmetic  1.68 us (1%)
    ppermute x4, waiting for transfers between devices, send_mixed(): return lax.ppermute(value, 'rcv', pairs)  39 us
    ppermute x4, starting transfers between devices, send_mixed(): return lax.ppermute(value, 'rcv', pairs)  32 us
    pallas_call x2, Pallas kernels, back_product(): pl.pallas_call(back_kernel, out_shape=(jax.ShapeDtypeStruct((samples, row...  13.2 us
    pallas_call x1, Pallas kernels, own_total(): pl.pallas_call(total_kernel, out_shape=jax.ShapeDtypeStruct((samples, row...  12.7 us
    ppermute x7, waiting for transfers between devices, send(): lax.ppermute(value, 'rcv', [(i, i ^ offset) for i in range(lax.axis_size(...  10.4 us
    ppermute x7, starting transfers between devices, send(): lax.ppermute(value, 'rcv', [(i, i ^ offset) for i in range(lax.axis_size(...  8.11 us
    another operation x1, loops' own time, meet_mixed(): lax.switch(low_offset - lowest, branches, near, mine, observed, first_mee...  7.37 us
    pallas_call x1, Pallas kernels, turn(): pl.pallas_call(turn_kernel, out_shape=jax.ShapeDtypeStruct((samples, rows...  5.42 us
  transfers between devices with their start and end apart: 11, of which 9 were waited for; matrix products, arithmetic and copies ran while one was open for 0% of the time, Pallas kernels for 22%

profile of v1, /device:TPU:0, one launch (start us, length us, event | category | flops | bytes accessed | tf_op | source)
XLA Modules:
  0.0 141.0 jit_solution(17141877920954131882)
XLA Ops:
  0.0 1.3 fusion.6
  3.2 112.7 %conditional.4 = ((f32[384,1024]{1,0:T(8,128)}, bf16[384,1024]{1,0:T(8,128)(2,1)}, bf16[384,1024]{1,0:T(8,128)(2,1)})) conditional(s32[]{:T(128)} %convert_element_type.3, (s32[]{:T(128)}, bf16[1024,384]{1,0:T(8,128)(2,1)}, s32[1]{0:T(128)}, bf16[2,1024,1024]{2,1,0:T(8,128)(2,1)}) %tuple.99, (s32[]{:T(128)}, s32[1]{0:T(128)}, ...), branch_computations={%region_0.15_spmd, %region_15.24_spmd} | conditional | flops 12 | bytes 28312046 | solution.py:392
  3.3 111.5 %conditional.2 = (f32[384,1024]{1,0:T(8,128)S(1)}, bf16[384,1024]{1,0:T(8,128)(2,1)}, bf16[384,1024]{1,0:T(8,128)(2,1)}) conditional(s32[]{:T(128)} %clamp.6, (bf16[1024,384]{1,0:T(8,128)(2,1)}, s32[1]{0:T(128)}, bf16[2,1024,1024]{2,1,0:T(8,128)(2,1)}) %tuple.89, (bf16[1024,384]{1,0:T(8,128)(2,1)}, s32[1]{0:T(128)}, ...), branch_computations={%region_16.16_spmd, %region_17.17_spmd, %region_18.18_spmd, %regio... | conditional | flops 1 | bytes 22020376 | solution.py:370
  10.6 4.1 %collective-permute-start.45 = (bf16[1024,384]{1,0:T(8,128)(2,1)}, bf16[1024,384]{1,0:T(8,128)(2,1)S(1)}, u32[]{:S(2)}, u32[]{:S(2)}) collective-permute-start(bf16[1024,384]{1,0:T(8,128)(2,1)} %get-tuple-element.241.rows_ref.mine_ref), channel_id=1, source_target_pairs={{0,12},{1,13},{2,14},{3,15},{4,8},{5,9},{6,10},{7,11},{8,27},{9,26... | collective-permute-start | bytes 2359304 | tf_op jit(solution)/shard_map/cond/branch_1_fun/cond/branch_4_fun/ppermute | solution.py:33
  15.2 5.4 %branch_4_fun.8.mine_t = bf16[384,1024]{1,0:T(8,128)(2,1)} custom-call(bf16[1024,384]{1,0:T(8,128)(2,1)} %get-tuple-element.241.rows_ref.mine_ref), custom_call_target="tpu_custom_call" | custom-call | tf_op jit(solution)/shard_map/cond/branch_1_fun/cond/branch_4_fun/pallas_call | solution.py:46
  20.6 12.3 %collective-permute-done.45.other_ref.second_ref = bf16[1024,384]{1,0:T(8,128)(2,1)S(1)} collective-permute-done((bf16[1024,384]{1,0:T(8,128)(2,1)}, bf16[1024,384]{1,0:T(8,128)(2,1)S(1)}, u32[]{:S(2)}, u32[]{:S(2)}) %collective-permute-start.45) | collective-permute-done | bytes 786464 | tf_op jit(solution)/shard_map/cond/branch_1_fun/cond/branch_4_fun/ppermute | solution.py:33
  33.8 6.6 %branch_4_fun.10 = (bf16[384,1024]{1,0:T(8,128)(2,1)}, bf16[1024,1024]{1,0:T(8,128)(2,1)}) custom-call(s32[1]{0:T(128)S(6)} %sub.29._, bf16[1024,384]{1,0:T(8,128)(2,1)S(1)} %copy-done.4, bf16[384,1024]{1,0:T(8,128)(2,1)} %branch_4_fun.8.mine_t, bf16[1024,384]{1,0:T(8,128)(2,1)} %copy-done.13, bf16[2,1024,1024]{2,1,0:T(8,128)(2,1)} %get-tuple-element.243.obs_ref), custom_call_target="tpu_custom_call" | custom-call | tf_op jit(solution)/shard_map/cond/branch_1_fun/cond/branch_4_fun/pallas_call | solution.py:260
  40.5 1.7 %collective-permute-start.47 = (bf16[384,1024]{1,0:T(8,128)(2,1)}, bf16[384,1024]{1,0:T(8,128)(2,1)}, u32[]{:S(2)}, u32[]{:S(2)}) collective-permute-start(bf16[384,1024]{1,0:T(8,128)(2,1)} %get-tuple-element.247), channel_id=1, source_target_pairs={{0,19},{1,18},{2,17},{3,16},{4,23},{5,22},{6,21},{7,20},{8,4},{9,5... | collective-permute-start | bytes 2359304 | tf_op jit(solution)/shard_map/cond/branch_1_fun/cond/branch_4_fun/ppermute | solution.py:33
  42.2 9.3 %collective-permute-done.44.other_ref.first_ref = bf16[1024,384]{1,0:T(8,128)(2,1)S(1)} collective-permute-done((bf16[1024,384]{1,0:T(8,128)(2,1)}, bf16[1024,384]{1,0:T(8,128)(2,1)S(1)}, u32[]{:S(2)}, u32[]{:S(2)}) %collective-permute-start.44) | collective-permute-done | bytes 786464 | tf_op jit(solution)/shard_map/cond/branch_1_fun/cond/branch_4_fun/ppermute | solution.py:33
  52.4 6.6 %branch_4_fun.9 = (bf16[384,1024]{1,0:T(8,128)(2,1)}, bf16[1024,1024]{1,0:T(8,128)(2,1)}) custom-call(s32[1]{0:T(128)} %get-tuple-element.242._, bf16[1024,384]{1,0:T(8,128)(2,1)S(1)} %copy-done.4, bf16[384,1024]{1,0:T(8,128)(2,1)} %branch_4_fun.8.mine_t, bf16[1024,384]{1,0:T(8,128)(2,1)} %copy-done.21, bf16[2,1024,1024]{2,1,0:T(8,128)(2,1)} %get-tuple-element.243.obs_ref), custom_call_target="tpu_custom_call" | custom-call | tf_op jit(solution)/shard_map/cond/branch_1_fun/cond/branch_4_fun/pallas_call | solution.py:260
  59.0 25.7 %collective-permute-start.46 = (bf16[384,1024]{1,0:T(8,128)(2,1)}, bf16[384,1024]{1,0:T(8,128)(2,1)}, u32[]{:S(2)}, u32[]{:S(2)}) collective-permute-start(bf16[384,1024]{1,0:T(8,128)(2,1)} %get-tuple-element.246), channel_id=1, source_target_pairs={{0,12},{1,13},{2,14},{3,15},{4,8},{5,9},{6,10},{7,11},{8,27},{9,26... | collective-permute-start | bytes 2359304 | tf_op jit(solution)/shard_map/cond/branch_1_fun/cond/branch_4_fun/ppermute | solution.py:33
  84.7 12.7 %branch_4_fun.11 = f32[384,1024]{1,0:T(8,128)S(1)} custom-call(bf16[1024,384]{1,0:T(8,128)(2,1)} %copy-done.21, bf16[1024,384]{1,0:T(8,128)(2,1)} %copy-done.13, bf16[1024,1024]{1,0:T(8,128)(2,1)} %get-tuple-element.244.first_weights, bf16[1024,1024]{1,0:T(8,128)(2,1)} %get-tuple-element.245.second_weights), custom_call_target="tpu_custom_call" | custom-call | tf_op jit(solution)/shard_map/cond/branch_1_fun/cond/branch_4_fun/pallas_call | solution.py:302
  97.4 14.7 %collective-permute-done.47 = bf16[384,1024]{1,0:T(8,128)(2,1)} collective-permute-done((bf16[384,1024]{1,0:T(8,128)(2,1)}, bf16[384,1024]{1,0:T(8,128)(2,1)}, u32[]{:S(2)}, u32[]{:S(2)}) %collective-permute-start.47) | collective-permute-done | bytes 786464 | tf_op jit(solution)/shard_map/cond/branch_1_fun/cond/branch_4_fun/ppermute | solution.py:33
  112.1 2.6 %collective-permute-done.46 = bf16[384,1024]{1,0:T(8,128)(2,1)} collective-permute-done((bf16[384,1024]{1,0:T(8,128)(2,1)}, bf16[384,1024]{1,0:T(8,128)(2,1)}, u32[]{:S(2)}, u32[]{:S(2)}) %collective-permute-start.46) | collective-permute-done | bytes 786464 | tf_op jit(solution)/shard_map/cond/branch_1_fun/cond/branch_4_fun/ppermute | solution.py:33
  114.8 1.2 copy-done.8
  115.9 4.8 %shard_map.67 = (f32[256,384]{1,0:T(8,128)}, f32[256,384]{1,0:T(8,128)}) custom-call(s32[1]{0:T(128)} %bitcast.1.here_ref, f32[384,1024]{1,0:T(8,128)} %get-tuple-element.278.own_ref, bf16[384,1024]{1,0:T(8,128)(2,1)} %get-tuple-element.279.far_ref, bf16[384,1024]{1,0:T(8,128)(2,1)} %get-tuple-element.280.near_ref, bf16[1024,512]{1,0:T(8,128)(2,1)} %green_ref.1), custom_call_target="tpu_custom_call" | custom-call | tf_op jit(solution)/shard_map/pallas_call | solution.py:209
  120.8 1.8 %collective-permute-done.60 = f32[256,384]{1,0:T(8,128)S(1)} collective-permute-done((f32[256,384]{1,0:T(8,128)}, f32[256,384]{1,0:T(8,128)S(1)}, u32[]{:S(2)}, u32[]{:S(2)}) %collective-permute-start.60) | collective-permute-done | bytes 393248 | tf_op jit(solution)/shard_map/ppermute | solution.py:21
  123.8 1.5 %collective-permute-start.62 = (f32[64,384]{1,0:T(8,128)S(1)}, f32[64,384]{1,0:T(8,128)S(1)}, u32[]{:S(2)}, u32[]{:S(2)}) collective-permute-start(f32[64,384]{1,0:T(8,128)S(1)} %get-tuple-element.285), channel_id=1, source_target_pairs={{0,4},{1,5},{2,6},{3,7},{4,0},{5,1},{6,2},{7,3},{8,12},{9,13},{10,... | collective-permute-start | bytes 294920 | tf_op jit(solution)/shard_map/ppermute | solution.py:21
  125.3 1.9 %collective-permute-start.63 = (f32[64,384]{1,0:T(8,128)S(1)}, f32[64,384]{1,0:T(8,128)S(1)}, u32[]{:S(2)}, u32[]{:S(2)}) collective-permute-start(f32[64,384]{1,0:T(8,128)S(1)} %get-tuple-element.284), channel_id=1, source_target_pairs={{0,6},{1,7},{2,4},{3,5},{4,2},{5,3},{6,0},{7,1},{8,14},{9,15},{10,... | collective-permute-start | bytes 294920 | tf_op jit(solution)/shard_map/ppermute | solution.py:21
  127.3 2.2 %collective-permute-done.61 = f32[64,384]{1,0:T(8,128)S(1)} collective-permute-done((f32[64,384]{1,0:T(8,128)S(1)}, f32[64,384]{1,0:T(8,128)S(1)}, u32[]{:S(2)}, u32[]{:S(2)}) %collective-permute-start.61) | collective-permute-done | bytes 98336 | tf_op jit(solution)/shard_map/ppermute | solution.py:21
  129.4 2.2 %collective-permute-done.63 = f32[64,384]{1,0:T(8,128)S(1)} collective-permute-done((f32[64,384]{1,0:T(8,128)S(1)}, f32[64,384]{1,0:T(8,128)S(1)}, u32[]{:S(2)}, u32[]{:S(2)}) %collective-permute-start.63) | collective-permute-done | bytes 98336 | tf_op jit(solution)/shard_map/ppermute | solution.py:21
  131.8 3.0 %collective-permute-start.65 = (f32[16,384]{1,0:T(8,128)S(1)}, f32[16,384]{1,0:T(8,128)S(1)}, u32[]{:S(2)}, u32[]{:S(2)}) collective-permute-start(f32[16,384]{1,0:T(8,128)S(1)} %get-tuple-element.288), channel_id=1, source_target_pairs={{0,16},{1,17},{2,18},{3,19},{4,20},{5,21},{6,22},{7,23},{8,24},{9,... | collective-permute-start | bytes 73736 | tf_op jit(solution)/shard_map/ppermute | solution.py:21
  134.7 1.4 collective-permute-start.66
  136.5 3.8 %collective-permute-done.66 = f32[16,384]{1,0:T(8,128)S(1)} collective-permute-done((f32[16,384]{1,0:T(8,128)S(1)}, f32[16,384]{1,0:T(8,128)S(1)}, u32[]{:S(2)}, u32[]{:S(2)}) %collective-permute-start.66) | collective-permute-done | bytes 24608 | tf_op jit(solution)/shard_map/ppermute | solution.py:21
  (19 shorter events, 4.7 us)
Async XLA Ops:
  10.6 23.2 %copy-start.4 = (bf16[1024,384]{1,0:T(8,128)(2,1)S(1)}, bf16[1024,384]{1,0:T(8,128)(2,1)}, u32[]{:S(2)}) copy-start(bf16[1024,384]{1,0:T(8,128)(2,1)} %get-tuple-element.241.rows_ref.mine_ref) | copy-start | bytes 2359300 | tf_op jit(solution)/shard_map/cond/branch_1_fun/cond
  10.6 22.3 %collective-permute-start.45 = (bf16[1024,384]{1,0:T(8,128)(2,1)}, bf16[1024,384]{1,0:T(8,128)(2,1)S(1)}, u32[]{:S(2)}, u32[]{:S(2)}) collective-permute-start(bf16[1024,384]{1,0:T(8,128)(2,1)} %get-tuple-element.241.rows_ref.mine_ref), channel_id=1, source_target_pairs={{0,12},{1,13},{2,14},{3,15},{4,8},{5,9},{6,10},{7,11},{8,27},{9,26... | collective-permute-start | bytes 2359304 | tf_op jit(solution)/shard_map/cond/branch_1_fun/cond/branch_4_fun/ppermute | solution.py:33
  14.7 36.8 %collective-permute-start.44 = (bf16[1024,384]{1,0:T(8,128)(2,1)}, bf16[1024,384]{1,0:T(8,128)(2,1)S(1)}, u32[]{:S(2)}, u32[]{:S(2)}) collective-permute-start(bf16[1024,384]{1,0:T(8,128)(2,1)} %get-tuple-element.241.rows_ref.mine_ref), channel_id=1, source_target_pairs={{0,19},{1,18},{2,17},{3,16},{4,23},{5,22},{6,21},{7,20},{8,4},{9,5... | collective-permute-start | bytes 2359304 | tf_op jit(solution)/shard_map/cond/branch_1_fun/cond/branch_4_fun/ppermute | solution.py:33
  32.9 0.9 copy-start.13
  40.5 71.7 %collective-permute-start.47 = (bf16[384,1024]{1,0:T(8,128)(2,1)}, bf16[384,1024]{1,0:T(8,128)(2,1)}, u32[]{:S(2)}, u32[]{:S(2)}) collective-permute-start(bf16[384,1024]{1,0:T(8,128)(2,1)} %get-tuple-element.247), channel_id=1, source_target_pairs={{0,19},{1,18},{2,17},{3,16},{4,23},{5,22},{6,21},{7,20},{8,4},{9,5... | collective-permute-start | bytes 2359304 | tf_op jit(solution)/shard_map/cond/branch_1_fun/cond/branch_4_fun/ppermute | solution.py:33
  51.5 0.9 copy-start.21
  59.0 55.7 %collective-permute-start.46 = (bf16[384,1024]{1,0:T(8,128)(2,1)}, bf16[384,1024]{1,0:T(8,128)(2,1)}, u32[]{:S(2)}, u32[]{:S(2)}) collective-permute-start(bf16[384,1024]{1,0:T(8,128)(2,1)} %get-tuple-element.246), channel_id=1, source_target_pairs={{0,12},{1,13},{2,14},{3,15},{4,8},{5,9},{6,10},{7,11},{8,27},{9,26... | collective-permute-start | bytes 2359304 | tf_op jit(solution)/shard_map/cond/branch_1_fun/cond/branch_4_fun/ppermute | solution.py:33
  114.7 1.2 copy-start.8
  120.7 1.9 %collective-permute-start.60 = (f32[256,384]{1,0:T(8,128)}, f32[256,384]{1,0:T(8,128)S(1)}, u32[]{:S(2)}, u32[]{:S(2)}) collective-permute-start(f32[256,384]{1,0:T(8,128)} %get-tuple-element.282), channel_id=1, source_target_pairs={{0,1},{1,0},{2,3},{3,2},{4,5},{5,4},{6,7},{7,6},{8,9},{9,8},{10,11... | collective-permute-start | bytes 1179656 | tf_op jit(solution)/shard_map/ppermute | solution.py:21
  123.7 5.7 %collective-permute-start.61 = (f32[64,384]{1,0:T(8,128)S(1)}, f32[64,384]{1,0:T(8,128)S(1)}, u32[]{:S(2)}, u32[]{:S(2)}) collective-permute-start(f32[64,384]{1,0:T(8,128)S(1)} %get-tuple-element.283), channel_id=1, source_target_pairs={{0,2},{1,3},{2,0},{3,1},{4,6},{5,7},{6,4},{7,5},{8,10},{9,11},{10,... | collective-permute-start | bytes 294920 | tf_op jit(solution)/shard_map/ppermute | solution.py:21
  123.8 5.7 %collective-permute-start.62 = (f32[64,384]{1,0:T(8,128)S(1)}, f32[64,384]{1,0:T(8,128)S(1)}, u32[]{:S(2)}, u32[]{:S(2)}) collective-permute-start(f32[64,384]{1,0:T(8,128)S(1)} %get-tuple-element.285), channel_id=1, source_target_pairs={{0,4},{1,5},{2,6},{3,7},{4,0},{5,1},{6,2},{7,3},{8,12},{9,13},{10,... | collective-permute-start | bytes 294920 | tf_op jit(solution)/shard_map/ppermute | solution.py:21
  125.3 6.3 %collective-permute-start.63 = (f32[64,384]{1,0:T(8,128)S(1)}, f32[64,384]{1,0:T(8,128)S(1)}, u32[]{:S(2)}, u32[]{:S(2)}) collective-permute-start(f32[64,384]{1,0:T(8,128)S(1)} %get-tuple-element.284), channel_id=1, source_target_pairs={{0,6},{1,7},{2,4},{3,5},{4,2},{5,3},{6,0},{7,1},{8,14},{9,15},{10,... | collective-permute-start | bytes 294920 | tf_op jit(solution)/shard_map/ppermute | solution.py:21
  131.7 4.5 %collective-permute-start.64 = (f32[16,384]{1,0:T(8,128)S(1)}, f32[16,384]{1,0:T(8,128)S(1)}, u32[]{:S(2)}, u32[]{:S(2)}) collective-permute-start(f32[16,384]{1,0:T(8,128)S(1)} %get-tuple-element.286), channel_id=1, source_target_pairs={{0,8},{1,9},{2,10},{3,11},{4,12},{5,13},{6,14},{7,15},{8,0},{9,1},... | collective-permute-start | bytes 73736 | tf_op jit(solution)/shard_map/ppermute | solution.py:21
  131.8 4.8 %collective-permute-start.65 = (f32[16,384]{1,0:T(8,128)S(1)}, f32[16,384]{1,0:T(8,128)S(1)}, u32[]{:S(2)}, u32[]{:S(2)}) collective-permute-start(f32[16,384]{1,0:T(8,128)S(1)} %get-tuple-element.288), channel_id=1, source_target_pairs={{0,16},{1,17},{2,18},{3,19},{4,20},{5,21},{6,22},{7,23},{8,24},{9,... | collective-permute-start | bytes 73736 | tf_op jit(solution)/shard_map/ppermute | solution.py:21
  134.7 5.6 %collective-permute-start.66 = (f32[16,384]{1,0:T(8,128)S(1)}, f32[16,384]{1,0:T(8,128)S(1)}, u32[]{:S(2)}, u32[]{:S(2)}) collective-permute-start(f32[16,384]{1,0:T(8,128)S(1)} %get-tuple-element.287), channel_id=1, source_target_pairs={{0,24},{1,25},{2,26},{3,27},{4,28},{5,29},{6,30},{7,31},{8,16},{9,... | collective-permute-start | bytes 73736 | tf_op jit(solution)/shard_map/ppermute | solution.py:21

commit v2 on v1

--- a/solution.py
+++ b/solution.py
@@ -174,29 +174,39 @@
     )(far, near, even_weights, odd_weights)
 
 
-def partial_kernel(order, here_ref, own_ref, far_ref, near_ref, green_ref, *outs_and_scratch):
-    outs, (total, turned) = outs_and_scratch[:-2], outs_and_scratch[-2:]
-    chunk = pl.program_id(0)
-    adjoint = own_ref[...] + far_ref[...].astype(f32) + near_ref[...].astype(f32)
-    product = jnp.dot(adjoint.astype(jnp.bfloat16), green_ref[...], preferred_element_type=f32)
-
-    @pl.when(chunk == 0)
-    def _():
-        total[...] = product
-
-    @pl.when(chunk > 0)
-    def _():
-        total[...] += product
-
-    @pl.when(chunk == pl.num_programs(0) - 1)
-    def _():
-        turned[...] = total[...].T
-        block = turned.shape[0] // len(order)
-        each = len(order) // len(outs)
-        for place, index in enumerate(order):
-            source = pl.multiple_of((here_ref[0] ^ index) * block, block)
-            spot = place % each * block
-            outs[place // each][spot : spot + block, :] = turned[pl.ds(source, block), :]
+def partial_kernel(order, here_ref, own, far, near, green, *refs):
+    outs, (own_in, far_in, near_in, green_in, total, turned, sems) = refs[:-7], refs[-7:]
+    chunks = own.shape[1] // chunk_rows
+    copies = []
+    for chunk in range(chunks):
+        columns = pl.ds(chunk * chunk_rows, chunk_rows)
+        moves = [(own, own_in), (far, far_in), (near, near_in)]
+        views = [(source.at[:, columns], held.at[:, columns]) for source, held in moves]
+        views.append((green.at[columns], green_in.at[columns]))
+        copies.append(
+            [
+                pltpu.make_async_copy(source, held, sems.at[chunk, place])
+                for place, (source, held) in enumerate(views)
+            ]
+        )
+    for batch in copies:
+        for copy in batch:
+            copy.start()
+    for chunk, batch in enumerate(copies):
+        for copy in batch:
+            copy.wait()
+        columns = slice(chunk * chunk_rows, (chunk + 1) * chunk_rows)
+        adjoint = own_in[:, columns] + far_in[:, columns].astype(f32)
+        adjoint = (adjoint + near_in[:, columns].astype(f32)).astype(jnp.bfloat16)
+        product = jnp.dot(adjoint, green_in[columns], preferred_element_type=f32)
+        total[...] = product if chunk == 0 else total[...] + product
+    turned[...] = total[...].T
+    block = turned.shape[0] // len(order)
+    each = len(order) // len(outs)
+    for place, index in enumerate(order):
+        source = pl.multiple_of((here_ref[0] ^ index) * block, block)
+        spot = place % each * block
+        outs[place // each][spot : spot + block, :] = turned[pl.ds(source, block), :]
 
 
 def partial_gradient(here, own, far_return, near_return, green_block, order, parts):
@@ -204,19 +214,22 @@
     cells = green_block.shape[1]
     natural = cells // len(order) % 8 != 0
     kernel_order, kernel_parts = ([0], 1) if natural else (order, parts)
-    column = pl.BlockSpec((samples, chunk_rows), lambda c, here: (0, c))
     size = cells // kernel_parts
     outs = pl.pallas_call(
         functools.partial(partial_kernel, kernel_order),
         out_shape=[jax.ShapeDtypeStruct((size, samples), f32)] * kernel_parts,
-        grid_spec=pltpu.PrefetchScalarGridSpec(
-            num_scalar_prefetch=1,
-            grid=(rows // chunk_rows,),
-            in_specs=[column] * 3 + [pl.BlockSpec((chunk_rows, cells), lambda c, here: (c, 0))],
-            out_specs=[pl.BlockSpec((size, samples), lambda c, here: (0, 0))] * kernel_parts,
-            scratch_shapes=[pltpu.VMEM((samples, cells), f32), pltpu.VMEM((cells, samples), f32)],
-        ),
-        compiler_params=pltpu.CompilerParams(dimension_semantics=("arbitrary",)),
+        in_specs=[pl.BlockSpec(memory_space=pltpu.SMEM)]
+        + [pl.BlockSpec(memory_space=pltpu.HBM)] * 4,
+        out_specs=[pl.BlockSpec(memory_space=pltpu.VMEM)] * kernel_parts,
+        scratch_shapes=[
+            pltpu.VMEM((samples, rows), f32),
+            pltpu.VMEM((samples, rows), jnp.bfloat16),
+            pltpu.VMEM((samples, rows), jnp.bfloat16),
+            pltpu.VMEM((rows, cells), jnp.bfloat16),
+            pltpu.VMEM((samples, cells), f32),
+            pltpu.VMEM((cells, samples), f32),
+            pltpu.SemaphoreType.DMA((rows // chunk_rows, 4)),
+        ],
     )(here * 0 if natural else here, own, far_return, near_return, green_block)
     if natural:
         blocks = outs[0].reshape(len(order), cells // len(order), samples)
@@ -419,14 +432,17 @@
 
 def scatter_sum(parts, groups):
     total = None
-    for level, width in groups:
+    for stage, (level, width) in enumerate(groups):
         if total is not None:
             size = total.shape[0] >> width
             parts = [total[digit * size : (digit + 1) * size] for digit in range(1 << width)]
-        moved = [send(parts[digit], digit << level) for digit in range(1, 1 << width)]
+        kind = jnp.bfloat16 if stage == 1 else f32
+        moved = [
+            send(parts[digit].astype(kind), digit << level) for digit in range(1, 1 << width)
+        ]
         total = parts[0]
         for piece in moved:
-            total = total + piece
+            total = total + piece.astype(f32)
     return total
 
 

time: 142 us -> 140 us (0.986)
  no operation moved by 1% of the time
where the time goes in v2:
time: 140 us; the launch traced here: 139 us
  waiting for transfers between devices  48.9 us (35%)
  starting transfers between devices  40.1 us (29%)
  Pallas kernels  35.1 us (25%)
  loops' own time  7.41 us (5%)
  local copies, waits for them, and re-layouts  4.26 us (3%)
  between operations  1.93 us (1%)
  other arithmetic  1.68 us (1%)
    ppermute x4, waiting for transfers between devices, send_mixed(): return lax.ppermute(value, 'rcv', pairs)  39 us
    ppermute x4, starting transfers between devices, send_mixed(): return lax.ppermute(value, 'rcv', pairs)  32 us
    pallas_call x2, Pallas kernels, back_product(): pl.pallas_call(back_kernel, out_shape=(jax.ShapeDtypeStruct((samples, row...  13.3 us
    pallas_call x1, Pallas kernels, own_total(): pl.pallas_call(total_kernel, out_shape=jax.ShapeDtypeStruct((samples, row...  12.7 us
    ppermute x7, waiting for transfers between devices, send(): lax.ppermute(value, 'rcv', [(i, i ^ offset) for i in range(lax.axis_size(...  9.88 us
    ppermute x7, starting transfers between devices, send(): lax.ppermute(value, 'rcv', [(i, i ^ offset) for i in range(lax.axis_size(...  8.17 us
    another operation x1, loops' own time, meet_mixed(): lax.switch(low_offset - lowest, branches, near, mine, observed, first_mee...  7.37 us
    pallas_call x1, Pallas kernels, turn(): pl.pallas_call(turn_kernel, out_shape=jax.ShapeDtypeStruct((samples, rows...  5.42 us
  transfers between devices with their start and end apart: 11, of which 9 were waited for; matrix products, arithmetic and copies ran while one was open for 0% of the time, Pallas kernels for 22%

profile of v2, /device:TPU:0, one launch (start us, length us, event | category | flops | bytes accessed | tf_op | source)
XLA Modules:
  0.0 139.4 jit_solution(241220963519040282)
XLA Ops:
  0.0 1.3 fusion.7
  3.2 112.7 %conditional.4 = ((f32[384,1024]{1,0:T(8,128)}, bf16[384,1024]{1,0:T(8,128)(2,1)}, bf16[384,1024]{1,0:T(8,128)(2,1)})) conditional(s32[]{:T(128)} %convert_element_type.15, (s32[]{:T(128)}, bf16[1024,384]{1,0:T(8,128)(2,1)}, s32[1]{0:T(128)}, bf16[2,1024,1024]{2,1,0:T(8,128)(2,1)}) %tuple.99, (s32[]{:T(128)}, s32[1]{0:T(128)}, ...), branch_computations={%region_0.15_spmd, %region_15.24_spmd} | conditional | flops 12 | bytes 28312046 | solution.py:405
  3.2 111.5 %conditional.2 = (f32[384,1024]{1,0:T(8,128)S(1)}, bf16[384,1024]{1,0:T(8,128)(2,1)}, bf16[384,1024]{1,0:T(8,128)(2,1)}) conditional(s32[]{:T(128)} %clamp.6, (bf16[1024,384]{1,0:T(8,128)(2,1)}, s32[1]{0:T(128)}, bf16[2,1024,1024]{2,1,0:T(8,128)(2,1)}) %tuple.89, (bf16[1024,384]{1,0:T(8,128)(2,1)}, s32[1]{0:T(128)}, ...), branch_computations={%region_16.16_spmd, %region_17.17_spmd, %region_18.18_spmd, %regio... | conditional | flops 1 | bytes 22020376 | solution.py:383
  10.6 4.1 %collective-permute-start.45 = (bf16[1024,384]{1,0:T(8,128)(2,1)}, bf16[1024,384]{1,0:T(8,128)(2,1)S(1)}, u32[]{:S(2)}, u32[]{:S(2)}) collective-permute-start(bf16[1024,384]{1,0:T(8,128)(2,1)} %get-tuple-element.241.rows_ref.mine_ref), channel_id=1, source_target_pairs={{0,12},{1,13},{2,14},{3,15},{4,8},{5,9},{6,10},{7,11},{8,27},{9,26... | collective-permute-start | bytes 2359304 | tf_op jit(solution)/shard_map/cond/branch_1_fun/cond/branch_4_fun/ppermute | solution.py:33
  15.1 5.4 %branch_4_fun.8.mine_t = bf16[384,1024]{1,0:T(8,128)(2,1)} custom-call(bf16[1024,384]{1,0:T(8,128)(2,1)} %get-tuple-element.241.rows_ref.mine_ref), custom_call_target="tpu_custom_call" | custom-call | tf_op jit(solution)/shard_map/cond/branch_1_fun/cond/branch_4_fun/pallas_call | solution.py:46
  20.6 12.3 %collective-permute-done.45.other_ref.second_ref = bf16[1024,384]{1,0:T(8,128)(2,1)S(1)} collective-permute-done((bf16[1024,384]{1,0:T(8,128)(2,1)}, bf16[1024,384]{1,0:T(8,128)(2,1)S(1)}, u32[]{:S(2)}, u32[]{:S(2)}) %collective-permute-start.45) | collective-permute-done | bytes 786464 | tf_op jit(solution)/shard_map/cond/branch_1_fun/cond/branch_4_fun/ppermute | solution.py:33
  33.8 6.6 %branch_4_fun.10 = (bf16[384,1024]{1,0:T(8,128)(2,1)}, bf16[1024,1024]{1,0:T(8,128)(2,1)}) custom-call(s32[1]{0:T(128)S(6)} %sub.29._, bf16[1024,384]{1,0:T(8,128)(2,1)S(1)} %copy-done.4, bf16[384,1024]{1,0:T(8,128)(2,1)} %branch_4_fun.8.mine_t, bf16[1024,384]{1,0:T(8,128)(2,1)} %copy-done.13, bf16[2,1024,1024]{2,1,0:T(8,128)(2,1)} %get-tuple-element.243.obs_ref), custom_call_target="tpu_custom_call" | custom-call | tf_op jit(solution)/shard_map/cond/branch_1_fun/cond/branch_4_fun/pallas_call | solution.py:273
  40.4 1.7 %collective-permute-start.47 = (bf16[384,1024]{1,0:T(8,128)(2,1)}, bf16[384,1024]{1,0:T(8,128)(2,1)}, u32[]{:S(2)}, u32[]{:S(2)}) collective-permute-start(bf16[384,1024]{1,0:T(8,128)(2,1)} %get-tuple-element.247), channel_id=1, source_target_pairs={{0,19},{1,18},{2,17},{3,16},{4,23},{5,22},{6,21},{7,20},{8,4},{9,5... | collective-permute-start | bytes 2359304 | tf_op jit(solution)/shard_map/cond/branch_1_fun/cond/branch_4_fun/ppermute | solution.py:33
  42.1 9.3 %collective-permute-done.44.other_ref.first_ref = bf16[1024,384]{1,0:T(8,128)(2,1)S(1)} collective-permute-done((bf16[1024,384]{1,0:T(8,128)(2,1)}, bf16[1024,384]{1,0:T(8,128)(2,1)S(1)}, u32[]{:S(2)}, u32[]{:S(2)}) %collective-permute-start.44) | collective-permute-done | bytes 786464 | tf_op jit(solution)/shard_map/cond/branch_1_fun/cond/branch_4_fun/ppermute | solution.py:33
  52.3 6.6 %branch_4_fun.9 = (bf16[384,1024]{1,0:T(8,128)(2,1)}, bf16[1024,1024]{1,0:T(8,128)(2,1)}) custom-call(s32[1]{0:T(128)} %get-tuple-element.242._, bf16[1024,384]{1,0:T(8,128)(2,1)S(1)} %copy-done.4, bf16[384,1024]{1,0:T(8,128)(2,1)} %branch_4_fun.8.mine_t, bf16[1024,384]{1,0:T(8,128)(2,1)} %copy-done.21, bf16[2,1024,1024]{2,1,0:T(8,128)(2,1)} %get-tuple-element.243.obs_ref), custom_call_target="tpu_custom_call" | custom-call | tf_op jit(solution)/shard_map/cond/branch_1_fun/cond/branch_4_fun/pallas_call | solution.py:273
  58.9 25.7 %collective-permute-start.46 = (bf16[384,1024]{1,0:T(8,128)(2,1)}, bf16[384,1024]{1,0:T(8,128)(2,1)}, u32[]{:S(2)}, u32[]{:S(2)}) collective-permute-start(bf16[384,1024]{1,0:T(8,128)(2,1)} %get-tuple-element.246), channel_id=1, source_target_pairs={{0,12},{1,13},{2,14},{3,15},{4,8},{5,9},{6,10},{7,11},{8,27},{9,26... | collective-permute-start | bytes 2359304 | tf_op jit(solution)/shard_map/cond/branch_1_fun/cond/branch_4_fun/ppermute | solution.py:33
  84.6 12.7 %branch_4_fun.11 = f32[384,1024]{1,0:T(8,128)S(1)} custom-call(bf16[1024,384]{1,0:T(8,128)(2,1)} %copy-done.21, bf16[1024,384]{1,0:T(8,128)(2,1)} %copy-done.13, bf16[1024,1024]{1,0:T(8,128)(2,1)} %get-tuple-element.244.first_weights, bf16[1024,1024]{1,0:T(8,128)(2,1)} %get-tuple-element.245.second_weights), custom_call_target="tpu_custom_call" | custom-call | tf_op jit(solution)/shard_map/cond/branch_1_fun/cond/branch_4_fun/pallas_call | solution.py:315
  97.3 14.7 %collective-permute-done.47 = bf16[384,1024]{1,0:T(8,128)(2,1)} collective-permute-done((bf16[384,1024]{1,0:T(8,128)(2,1)}, bf16[384,1024]{1,0:T(8,128)(2,1)}, u32[]{:S(2)}, u32[]{:S(2)}) %collective-permute-start.47) | collective-permute-done | bytes 786464 | tf_op jit(solution)/shard_map/cond/branch_1_fun/cond/branch_4_fun/ppermute | solution.py:33
  112.1 2.6 %collective-permute-done.46 = bf16[384,1024]{1,0:T(8,128)(2,1)} collective-permute-done((bf16[384,1024]{1,0:T(8,128)(2,1)}, bf16[384,1024]{1,0:T(8,128)(2,1)}, u32[]{:S(2)}, u32[]{:S(2)}) %collective-permute-start.46) | collective-permute-done | bytes 786464 | tf_op jit(solution)/shard_map/cond/branch_1_fun/cond/branch_4_fun/ppermute | solution.py:33
  114.7 1.2 copy-done.8
  115.9 3.7 %shard_map.67 = (f32[256,384]{1,0:T(8,128)}, f32[256,384]{1,0:T(8,128)}) custom-call(s32[1]{0:T(128)} %bitcast.1.here_ref, f32[384,1024]{1,0:T(8,128)} %get-tuple-element.278.own, bf16[384,1024]{1,0:T(8,128)(2,1)} %get-tuple-element.279.far, bf16[384,1024]{1,0:T(8,128)(2,1)} %get-tuple-element.280.near, bf16[1024,512]{1,0:T(8,128)(2,1)} %green.1), custom_call_target="tpu_custom_call" | custom-call | tf_op jit(solution)/shard_map/pallas_call | solution.py:218
  119.8 1.8 %collective-permute-done.60 = f32[256,384]{1,0:T(8,128)S(1)} collective-permute-done((f32[256,384]{1,0:T(8,128)}, f32[256,384]{1,0:T(8,128)S(1)}, u32[]{:S(2)}, u32[]{:S(2)}) %collective-permute-start.60) | collective-permute-done | bytes 393248 | tf_op jit(solution)/shard_map/ppermute | solution.py:21
  121.6 1.0 fusion.4
  122.7 1.5 %collective-permute-start.62 = (bf16[64,384]{1,0:T(8,128)(2,1)S(1)}, bf16[64,384]{1,0:T(8,128)(2,1)S(1)}, u32[]{:S(2)}, u32[]{:S(2)}) collective-permute-start(bf16[64,384]{1,0:T(8,128)(2,1)S(1)} %get-tuple-element.287), channel_id=1, source_target_pairs={{0,4},{1,5},{2,6},{3,7},{4,0},{5,1},{6,2},{7,3},{8,12},{9,13},{10,... | collective-permute-start | bytes 147464 | tf_op jit(solution)/shard_map/ppermute | solution.py:21
  124.3 1.9 %collective-permute-start.63 = (bf16[64,384]{1,0:T(8,128)(2,1)S(1)}, bf16[64,384]{1,0:T(8,128)(2,1)S(1)}, u32[]{:S(2)}, u32[]{:S(2)}) collective-permute-start(bf16[64,384]{1,0:T(8,128)(2,1)S(1)} %get-tuple-element.286), channel_id=1, source_target_pairs={{0,6},{1,7},{2,4},{3,5},{4,2},{5,3},{6,0},{7,1},{8,14},{9,15},{10,... | collective-permute-start | bytes 147464 | tf_op jit(solution)/shard_map/ppermute | solution.py:21
  126.9 2.3 %collective-permute-done.63 = bf16[64,384]{1,0:T(8,128)(2,1)S(1)} collective-permute-done((bf16[64,384]{1,0:T(8,128)(2,1)S(1)}, bf16[64,384]{1,0:T(8,128)(2,1)S(1)}, u32[]{:S(2)}, u32[]{:S(2)}) %collective-permute-start.63) | collective-permute-done | bytes 49184 | tf_op jit(solution)/shard_map/ppermute | solution.py:21
  129.4 3.8 %collective-permute-start.65 = (f32[16,384]{1,0:T(8,128)S(1)}, f32[16,384]{1,0:T(8,128)S(1)}, u32[]{:S(2)}, u32[]{:S(2)}) collective-permute-start(f32[16,384]{1,0:T(8,128)S(1)} %get-tuple-element.290), channel_id=1, source_target_pairs={{0,16},{1,17},{2,18},{3,19},{4,20},{5,21},{6,22},{7,23},{8,24},{9,... | collective-permute-start | bytes 73736 | tf_op jit(solution)/shard_map/ppermute | solution.py:21
  133.8 1.2 collective-permute-done.65
  135.0 3.8 %collective-permute-done.66 = f32[16,384]{1,0:T(8,128)S(1)} collective-permute-done((f32[16,384]{1,0:T(8,128)S(1)}, f32[16,384]{1,0:T(8,128)S(1)}, u32[]{:S(2)}, u32[]{:S(2)}) %collective-permute-start.66) | collective-permute-done | bytes 24608 | tf_op jit(solution)/shard_map/ppermute | solution.py:21
  (19 shorter events, 4.6 us)
Async XLA Ops:
  10.6 23.2 %copy-start.4 = (bf16[1024,384]{1,0:T(8,128)(2,1)S(1)}, bf16[1024,384]{1,0:T(8,128)(2,1)}, u32[]{:S(2)}) copy-start(bf16[1024,384]{1,0:T(8,128)(2,1)} %get-tuple-element.241.rows_ref.mine_ref) | copy-start | bytes 2359300 | tf_op jit(solution)/shard_map/cond/branch_1_fun/cond
  10.6 22.3 %collective-permute-start.45 = (bf16[1024,384]{1,0:T(8,128)(2,1)}, bf16[1024,384]{1,0:T(8,128)(2,1)S(1)}, u32[]{:S(2)}, u32[]{:S(2)}) collective-permute-start(bf16[1024,384]{1,0:T(8,128)(2,1)} %get-tuple-element.241.rows_ref.mine_ref), channel_id=1, source_target_pairs={{0,12},{1,13},{2,14},{3,15},{4,8},{5,9},{6,10},{7,11},{8,27},{9,26... | collective-permute-start | bytes 2359304 | tf_op jit(solution)/shard_map/cond/branch_1_fun/cond/branch_4_fun/ppermute | solution.py:33
  14.6 36.8 %collective-permute-start.44 = (bf16[1024,384]{1,0:T(8,128)(2,1)}, bf16[1024,384]{1,0:T(8,128)(2,1)S(1)}, u32[]{:S(2)}, u32[]{:S(2)}) collective-permute-start(bf16[1024,384]{1,0:T(8,128)(2,1)} %get-tuple-element.241.rows_ref.mine_ref), channel_id=1, source_target_pairs={{0,19},{1,18},{2,17},{3,16},{4,23},{5,22},{6,21},{7,20},{8,4},{9,5... | collective-permute-start | bytes 2359304 | tf_op jit(solution)/shard_map/cond/branch_1_fun/cond/branch_4_fun/ppermute | solution.py:33
  32.9 0.9 copy-start.13
  40.4 71.7 %collective-permute-start.47 = (bf16[384,1024]{1,0:T(8,128)(2,1)}, bf16[384,1024]{1,0:T(8,128)(2,1)}, u32[]{:S(2)}, u32[]{:S(2)}) collective-permute-start(bf16[384,1024]{1,0:T(8,128)(2,1)} %get-tuple-element.247), channel_id=1, source_target_pairs={{0,19},{1,18},{2,17},{3,16},{4,23},{5,22},{6,21},{7,20},{8,4},{9,5... | collective-permute-start | bytes 2359304 | tf_op jit(solution)/shard_map/cond/branch_1_fun/cond/branch_4_fun/ppermute | solution.py:33
  51.4 0.9 copy-start.21
  58.9 55.8 %collective-permute-start.46 = (bf16[384,1024]{1,0:T(8,128)(2,1)}, bf16[384,1024]{1,0:T(8,128)(2,1)}, u32[]{:S(2)}, u32[]{:S(2)}) collective-permute-start(bf16[384,1024]{1,0:T(8,128)(2,1)} %get-tuple-element.246), channel_id=1, source_target_pairs={{0,12},{1,13},{2,14},{3,15},{4,8},{5,9},{6,10},{7,11},{8,27},{9,26... | collective-permute-start | bytes 2359304 | tf_op jit(solution)/shard_map/cond/branch_1_fun/cond/branch_4_fun/ppermute | solution.py:33
  114.7 1.2 copy-start.8
  119.6 2.0 %collective-permute-start.60 = (f32[256,384]{1,0:T(8,128)}, f32[256,384]{1,0:T(8,128)S(1)}, u32[]{:S(2)}, u32[]{:S(2)}) collective-permute-start(f32[256,384]{1,0:T(8,128)} %get-tuple-element.282), channel_id=1, source_target_pairs={{0,1},{1,0},{2,3},{3,2},{4,5},{5,4},{6,7},{7,6},{8,9},{9,8},{10,11... | collective-permute-start | bytes 1179656 | tf_op jit(solution)/shard_map/ppermute | solution.py:21
  122.7 4.2 %collective-permute-start.61 = (bf16[64,384]{1,0:T(8,128)(2,1)S(1)}, bf16[64,384]{1,0:T(8,128)(2,1)S(1)}, u32[]{:S(2)}, u32[]{:S(2)}) collective-permute-start(bf16[64,384]{1,0:T(8,128)(2,1)S(1)} %get-tuple-element.285), channel_id=1, source_target_pairs={{0,2},{1,3},{2,0},{3,1},{4,6},{5,7},{6,4},{7,5},{8,10},{9,11},{10,... | collective-permute-start | bytes 147464 | tf_op jit(solution)/shard_map/ppermute | solution.py:21
  122.7 4.2 %collective-permute-start.62 = (bf16[64,384]{1,0:T(8,128)(2,1)S(1)}, bf16[64,384]{1,0:T(8,128)(2,1)S(1)}, u32[]{:S(2)}, u32[]{:S(2)}) collective-permute-start(bf16[64,384]{1,0:T(8,128)(2,1)S(1)} %get-tuple-element.287), channel_id=1, source_target_pairs={{0,4},{1,5},{2,6},{3,7},{4,0},{5,1},{6,2},{7,3},{8,12},{9,13},{10,... | collective-permute-start | bytes 147464 | tf_op jit(solution)/shard_map/ppermute | solution.py:21
  124.3 5.0 %collective-permute-start.63 = (bf16[64,384]{1,0:T(8,128)(2,1)S(1)}, bf16[64,384]{1,0:T(8,128)(2,1)S(1)}, u32[]{:S(2)}, u32[]{:S(2)}) collective-permute-start(bf16[64,384]{1,0:T(8,128)(2,1)S(1)} %get-tuple-element.286), channel_id=1, source_target_pairs={{0,6},{1,7},{2,4},{3,5},{4,2},{5,3},{6,0},{7,1},{8,14},{9,15},{10,... | collective-permute-start | bytes 147464 | tf_op jit(solution)/shard_map/ppermute | solution.py:21
  129.3 4.5 %collective-permute-start.64 = (f32[16,384]{1,0:T(8,128)S(1)}, f32[16,384]{1,0:T(8,128)S(1)}, u32[]{:S(2)}, u32[]{:S(2)}) collective-permute-start(f32[16,384]{1,0:T(8,128)S(1)} %get-tuple-element.288), channel_id=1, source_target_pairs={{0,8},{1,9},{2,10},{3,11},{4,12},{5,13},{6,14},{7,15},{8,0},{9,1},... | collective-permute-start | bytes 73736 | tf_op jit(solution)/shard_map/ppermute | solution.py:21
  129.4 5.6 %collective-permute-start.65 = (f32[16,384]{1,0:T(8,128)S(1)}, f32[16,384]{1,0:T(8,128)S(1)}, u32[]{:S(2)}, u32[]{:S(2)}) collective-permute-start(f32[16,384]{1,0:T(8,128)S(1)} %get-tuple-element.290), channel_id=1, source_target_pairs={{0,16},{1,17},{2,18},{3,19},{4,20},{5,21},{6,22},{7,23},{8,24},{9,... | collective-permute-start | bytes 73736 | tf_op jit(solution)/shard_map/ppermute | solution.py:21
  133.2 5.6 %collective-permute-start.66 = (f32[16,384]{1,0:T(8,128)S(1)}, f32[16,384]{1,0:T(8,128)S(1)}, u32[]{:S(2)}, u32[]{:S(2)}) collective-permute-start(f32[16,384]{1,0:T(8,128)S(1)} %get-tuple-element.289), channel_id=1, source_target_pairs={{0,24},{1,25},{2,26},{3,27},{4,28},{5,29},{6,30},{7,31},{8,16},{9,... | collective-permute-start | bytes 73736 | tf_op jit(solution)/shard_map/ppermute | solution.py:21

commit v3 on v2

--- a/solution.py
+++ b/solution.py
@@ -10,7 +10,7 @@
 student_nu = 0.01
 direct_bits = 5
 chunk_rows = 256
-block_rows = 1024
+block_rows = 512
 turn_rows = 128
 f32 = jnp.float32
 
@@ -160,7 +160,7 @@
     double = 2 * chunk_rows
     return pl.pallas_call(
         functools.partial(own_kernel, steps),
-        out_shape=jax.ShapeDtypeStruct((samples, rows), f32),
+        out_shape=pltpu.HBM((samples, rows), f32),
         grid=(rows // chunk_rows, 2 * steps),
         in_specs=[
             pl.BlockSpec((double, samples), lambda c, s: (jnp.clip(s, 0, steps - 1), 0)),
@@ -217,7 +217,7 @@
     size = cells // kernel_parts
     outs = pl.pallas_call(
         functools.partial(partial_kernel, kernel_order),
-        out_shape=[jax.ShapeDtypeStruct((size, samples), f32)] * kernel_parts,
+        out_shape=[pltpu.VMEM((size, samples), f32)] * kernel_parts,
         in_specs=[pl.BlockSpec(memory_space=pltpu.SMEM)]
         + [pl.BlockSpec(memory_space=pltpu.HBM)] * 4,
         out_specs=[pl.BlockSpec(memory_space=pltpu.VMEM)] * kernel_parts,
@@ -314,7 +314,7 @@
     weights = pl.BlockSpec((chunk_rows, chunk_rows), lambda c, s: (c, s))
     return pl.pallas_call(
         total_kernel,
-        out_shape=jax.ShapeDtypeStruct((samples, rows), f32),
+        out_shape=pltpu.HBM((samples, rows), f32),
         grid=(rows // chunk_rows, rows // chunk_rows),
         in_specs=[values, values, weights, weights],
         out_specs=pl.BlockSpec((samples, chunk_rows), lambda c, s: (0, c)),

time: 140 us -> 139 us (level)
  waiting for transfers between devices: 48.9 us -> 41.3 us
  Pallas kernels: 35.1 us -> 41.5 us
  starting transfers between devices: 40.1 us -> 43.3 us
    ppermute x4, waiting for transfers between devices: 39 us -> 31.7 us  [send_mixed(): return lax.ppermute(value, 'rcv', pairs)]
    pallas_call x2, Pallas kernels: 13.3 us -> 19.5 us  [back_product(): pl.pallas_call(back_kernel, out_shape=(jax.ShapeDtypeStruct((samples, row...]
    ppermute x4, starting transfers between devices: 32 us -> 35.1 us  [send_mixed(): return lax.ppermute(value, 'rcv', pairs)]
    cond x8 -> x6, local copies, waits for them, and re-layouts: 2.94 us -> 1.85 us
  transfers between devices with their start and end apart: 11 -> 11, of which waited for: 9 -> 9; matrix products, arithmetic and copies ran while one was open for 0% -> 0% of each run, Pallas kernels for 22% -> 28%
where the time goes in v3:
time: 139 us; the launch traced here: 138 us
  starting transfers between devices  43.3 us (31%)
  Pallas kernels  41.5 us (30%)
  waiting for transfers between devices  41.3 us (30%)
  loops' own time  6.53 us (5%)
  local copies, waits for them, and re-layouts  3.16 us (2%)
  between operations  1.99 us (1%)
    ppermute x4, starting transfers between devices, send_mixed(): return lax.ppermute(value, 'rcv', pairs)  35.1 us
    ppermute x4, waiting for transfers between devices, send_mixed(): return lax.ppermute(value, 'rcv', pairs)  31.7 us
    pallas_call x2, Pallas kernels, back_product(): pl.pallas_call(back_kernel, out_shape=(jax.ShapeDtypeStruct((samples, row...  19.5 us
    pallas_call x1, Pallas kernels, own_total(): pl.pallas_call(total_kernel, out_shape=pltpu.HBM((samples, rows), f32), g...  13.8 us
    ppermute x7, waiting for transfers between devices, send(): lax.ppermute(value, 'rcv', [(i, i ^ offset) for i in range(lax.axis_size(...  9.67 us
    ppermute x7, starting transfers between devices, send(): lax.ppermute(value, 'rcv', [(i, i ^ offset) for i in range(lax.axis_size(...  8.17 us
    another operation x1, loops' own time, meet_mixed(): lax.switch(low_offset - lowest, branches, near, mine, observed, first_mee...  6.49 us
    pallas_call x1, Pallas kernels, turn(): pl.pallas_call(turn_kernel, out_shape=jax.ShapeDtypeStruct((samples, rows...  5.38 us
  transfers between devices with their start and end apart: 11, of which 9 were waited for; matrix products, arithmetic and copies ran while one was open for 0% of the time, Pallas kernels for 28%

profile of v3, /device:TPU:0, one launch (start us, length us, event | category | flops | bytes accessed | tf_op | source)
XLA Modules:
  0.0 138.5 jit_solution(1951267401881616883)
XLA Ops:
  0.0 1.3 fusion.7
  3.2 113.8 %conditional.4 = ((f32[384,1024]{1,0:T(8,128)}, bf16[384,1024]{1,0:T(8,128)(2,1)}, bf16[384,1024]{1,0:T(8,128)(2,1)})) conditional(s32[]{:T(128)} %convert_element_type.15, (s32[]{:T(128)}, bf16[1024,384]{1,0:T(8,128)(2,1)}, s32[1]{0:T(128)}, bf16[2,1024,1024]{2,1,0:T(8,128)(2,1)}) %tuple.99, (s32[]{:T(128)}, s32[1]{0:T(128)}, ...), branch_computations={%region_0.15_spmd, %region_15.24_spmd} | conditional | flops 12 | bytes 22020538 | solution.py:405
  3.3 113.8 %conditional.2 = (f32[384,1024]{1,0:T(8,128)}, bf16[384,1024]{1,0:T(8,128)(2,1)}, bf16[384,1024]{1,0:T(8,128)(2,1)}) conditional(s32[]{:T(128)} %clamp.6, (bf16[1024,384]{1,0:T(8,128)(2,1)}, s32[1]{0:T(128)}, bf16[2,1024,1024]{2,1,0:T(8,128)(2,1)}) %tuple.89, (bf16[1024,384]{1,0:T(8,128)(2,1)}, s32[1]{0:T(128)}, ...), branch_computations={%region_16.16_spmd, %region_17.17_spmd, %region_18.18_spmd, %regio... | conditional | flops 1 | bytes 22020376 | solution.py:383
  9.7 4.1 %collective-permute-start.45 = (bf16[1024,384]{1,0:T(8,128)(2,1)}, bf16[1024,384]{1,0:T(8,128)(2,1)S(1)}, u32[]{:S(2)}, u32[]{:S(2)}) collective-permute-start(bf16[1024,384]{1,0:T(8,128)(2,1)} %get-tuple-element.241.rows_ref.mine_ref), channel_id=1, source_target_pairs={{0,12},{1,13},{2,14},{3,15},{4,8},{5,9},{6,10},{7,11},{8,27},{9,26... | collective-permute-start | bytes 2359304 | tf_op jit(solution)/shard_map/cond/branch_1_fun/cond/branch_4_fun/ppermute | solution.py:33
  14.3 5.4 %branch_4_fun.8.mine_t = bf16[384,1024]{1,0:T(8,128)(2,1)} custom-call(bf16[1024,384]{1,0:T(8,128)(2,1)} %get-tuple-element.241.rows_ref.mine_ref), custom_call_target="tpu_custom_call" | custom-call | tf_op jit(solution)/shard_map/cond/branch_1_fun/cond/branch_4_fun/pallas_call | solution.py:46
  19.7 12.4 %collective-permute-done.45.other_ref.second_ref = bf16[1024,384]{1,0:T(8,128)(2,1)S(1)} collective-permute-done((bf16[1024,384]{1,0:T(8,128)(2,1)}, bf16[1024,384]{1,0:T(8,128)(2,1)S(1)}, u32[]{:S(2)}, u32[]{:S(2)}) %collective-permute-start.45) | collective-permute-done | bytes 786464 | tf_op jit(solution)/shard_map/cond/branch_1_fun/cond/branch_4_fun/ppermute | solution.py:33
  32.1 0.9 copy-done.12
  33.0 9.7 %branch_4_fun.10 = (bf16[384,1024]{1,0:T(8,128)(2,1)}, bf16[1024,1024]{1,0:T(8,128)(2,1)}) custom-call(s32[1]{0:T(128)S(6)} %sub.29._, bf16[1024,384]{1,0:T(8,128)(2,1)S(1)} %copy-done.4, bf16[384,1024]{1,0:T(8,128)(2,1)} %branch_4_fun.8.mine_t, bf16[1024,384]{1,0:T(8,128)(2,1)} %copy-done.12, bf16[2,1024,1024]{2,1,0:T(8,128)(2,1)} %get-tuple-element.243.obs_ref), custom_call_target="tpu_custom_call" | custom-call | tf_op jit(solution)/shard_map/cond/branch_1_fun/cond/branch_4_fun/pallas_call | solution.py:273
  42.7 1.7 %collective-permute-start.47 = (bf16[384,1024]{1,0:T(8,128)(2,1)}, bf16[384,1024]{1,0:T(8,128)(2,1)}, u32[]{:S(2)}, u32[]{:S(2)}) collective-permute-start(bf16[384,1024]{1,0:T(8,128)(2,1)} %get-tuple-element.247), channel_id=1, source_target_pairs={{0,19},{1,18},{2,17},{3,16},{4,23},{5,22},{6,21},{7,20},{8,4},{9,5... | collective-permute-start | bytes 2359304 | tf_op jit(solution)/shard_map/cond/branch_1_fun/cond/branch_4_fun/ppermute | solution.py:33
  44.5 6.1 %collective-permute-done.44.other_ref.first_ref = bf16[1024,384]{1,0:T(8,128)(2,1)S(1)} collective-permute-done((bf16[1024,384]{1,0:T(8,128)(2,1)}, bf16[1024,384]{1,0:T(8,128)(2,1)S(1)}, u32[]{:S(2)}, u32[]{:S(2)}) %collective-permute-start.44) | collective-permute-done | bytes 786464 | tf_op jit(solution)/shard_map/cond/branch_1_fun/cond/branch_4_fun/ppermute | solution.py:33
  50.6 0.9 copy-done.20
  51.5 9.7 %branch_4_fun.9 = (bf16[384,1024]{1,0:T(8,128)(2,1)}, bf16[1024,1024]{1,0:T(8,128)(2,1)}) custom-call(s32[1]{0:T(128)} %get-tuple-element.242._, bf16[1024,384]{1,0:T(8,128)(2,1)S(1)} %copy-done.4, bf16[384,1024]{1,0:T(8,128)(2,1)} %branch_4_fun.8.mine_t, bf16[1024,384]{1,0:T(8,128)(2,1)} %copy-done.20, bf16[2,1024,1024]{2,1,0:T(8,128)(2,1)} %get-tuple-element.243.obs_ref), custom_call_target="tpu_custom_call" | custom-call | tf_op jit(solution)/shard_map/cond/branch_1_fun/cond/branch_4_fun/pallas_call | solution.py:273
  61.2 28.8 %collective-permute-start.46 = (bf16[384,1024]{1,0:T(8,128)(2,1)}, bf16[384,1024]{1,0:T(8,128)(2,1)}, u32[]{:S(2)}, u32[]{:S(2)}) collective-permute-start(bf16[384,1024]{1,0:T(8,128)(2,1)} %get-tuple-element.246), channel_id=1, source_target_pairs={{0,12},{1,13},{2,14},{3,15},{4,8},{5,9},{6,10},{7,11},{8,27},{9,26... | collective-permute-start | bytes 2359304 | tf_op jit(solution)/shard_map/cond/branch_1_fun/cond/branch_4_fun/ppermute | solution.py:33
  90.1 13.8 %branch_4_fun.11 = f32[384,1024]{1,0:T(8,128)} custom-call(bf16[1024,384]{1,0:T(8,128)(2,1)} %copy-done.20, bf16[1024,384]{1,0:T(8,128)(2,1)} %copy-done.12, bf16[1024,1024]{1,0:T(8,128)(2,1)} %get-tuple-element.244.first_weights, bf16[1024,1024]{1,0:T(8,128)(2,1)} %get-tuple-element.245.second_weights), custom_call_target="tpu_custom_call" | custom-call | tf_op jit(solution)/shard_map/cond/branch_1_fun/cond/branch_4_fun/pallas_call | solution.py:315
  103.9 10.5 %collective-permute-done.47 = bf16[384,1024]{1,0:T(8,128)(2,1)} collective-permute-done((bf16[384,1024]{1,0:T(8,128)(2,1)}, bf16[384,1024]{1,0:T(8,128)(2,1)}, u32[]{:S(2)}, u32[]{:S(2)}) %collective-permute-start.47) | collective-permute-done | bytes 786464 | tf_op jit(solution)/shard_map/cond/branch_1_fun/cond/branch_4_fun/ppermute | solution.py:33
  114.4 2.6 %collective-permute-done.46 = bf16[384,1024]{1,0:T(8,128)(2,1)} collective-permute-done((bf16[384,1024]{1,0:T(8,128)(2,1)}, bf16[384,1024]{1,0:T(8,128)(2,1)}, u32[]{:S(2)}, u32[]{:S(2)}) %collective-permute-start.46) | collective-permute-done | bytes 786464 | tf_op jit(solution)/shard_map/cond/branch_1_fun/cond/branch_4_fun/ppermute | solution.py:33
  117.0 2.8 %shard_map.67 = (f32[256,384]{1,0:T(8,128)S(1)}, f32[256,384]{1,0:T(8,128)S(1)}) custom-call(s32[1]{0:T(128)} %bitcast.1.here_ref, f32[384,1024]{1,0:T(8,128)} %get-tuple-element.278.own, bf16[384,1024]{1,0:T(8,128)(2,1)} %get-tuple-element.279.far, bf16[384,1024]{1,0:T(8,128)(2,1)} %get-tuple-element.280.near, bf16[1024,512]{1,0:T(8,128)(2,1)} %green.1), custom_call_target="tpu_custom_call" | custom-call | tf_op jit(solution)/shard_map/pallas_call | solution.py:218
  120.1 1.6 %collective-permute-done.60 = f32[256,384]{1,0:T(8,128)S(1)} collective-permute-done((f32[256,384]{1,0:T(8,128)S(1)}, f32[256,384]{1,0:T(8,128)S(1)}, u32[]{:S(2)}, u32[]{:S(2)}) %collective-permute-start.60) | collective-permute-done | bytes 393248 | tf_op jit(solution)/shard_map/ppermute | solution.py:21
  121.8 1.5 %collective-permute-start.62 = (bf16[64,384]{1,0:T(8,128)(2,1)S(1)}, bf16[64,384]{1,0:T(8,128)(2,1)S(1)}, u32[]{:S(2)}, u32[]{:S(2)}) collective-permute-start(bf16[64,384]{1,0:T(8,128)(2,1)S(1)} %get-tuple-element.287), channel_id=1, source_target_pairs={{0,4},{1,5},{2,6},{3,7},{4,0},{5,1},{6,2},{7,3},{8,12},{9,13},{10,... | collective-permute-start | bytes 147464 | tf_op jit(solution)/shard_map/ppermute | solution.py:21
  123.4 1.9 %collective-permute-start.63 = (bf16[64,384]{1,0:T(8,128)(2,1)S(1)}, bf16[64,384]{1,0:T(8,128)(2,1)S(1)}, u32[]{:S(2)}, u32[]{:S(2)}) collective-permute-start(bf16[64,384]{1,0:T(8,128)(2,1)S(1)} %get-tuple-element.286), channel_id=1, source_target_pairs={{0,6},{1,7},{2,4},{3,5},{4,2},{5,3},{6,0},{7,1},{8,14},{9,15},{10,... | collective-permute-start | bytes 147464 | tf_op jit(solution)/shard_map/ppermute | solution.py:21
  126.0 2.3 %collective-permute-done.63 = bf16[64,384]{1,0:T(8,128)(2,1)S(1)} collective-permute-done((bf16[64,384]{1,0:T(8,128)(2,1)S(1)}, bf16[64,384]{1,0:T(8,128)(2,1)S(1)}, u32[]{:S(2)}, u32[]{:S(2)}) %collective-permute-start.63) | collective-permute-done | bytes 49184 | tf_op jit(solution)/shard_map/ppermute | solution.py:21
  128.5 3.8 %collective-permute-start.65 = (f32[16,384]{1,0:T(8,128)S(1)}, f32[16,384]{1,0:T(8,128)S(1)}, u32[]{:S(2)}, u32[]{:S(2)}) collective-permute-start(f32[16,384]{1,0:T(8,128)S(1)} %get-tuple-element.290), channel_id=1, source_target_pairs={{0,16},{1,17},{2,18},{3,19},{4,20},{5,21},{6,22},{7,23},{8,24},{9,... | collective-permute-start | bytes 73736 | tf_op jit(solution)/shard_map/ppermute | solution.py:21
  132.9 1.2 collective-permute-done.65
  134.0 3.8 %collective-permute-done.66 = f32[16,384]{1,0:T(8,128)S(1)} collective-permute-done((f32[16,384]{1,0:T(8,128)S(1)}, f32[16,384]{1,0:T(8,128)S(1)}, u32[]{:S(2)}, u32[]{:S(2)}) %collective-permute-start.66) | collective-permute-done | bytes 24608 | tf_op jit(solution)/shard_map/ppermute | solution.py:21
  (17 shorter events, 2.8 us)
Async XLA Ops:
  9.7 23.3 %copy-start.4 = (bf16[1024,384]{1,0:T(8,128)(2,1)S(1)}, bf16[1024,384]{1,0:T(8,128)(2,1)}, u32[]{:S(2)}) copy-start(bf16[1024,384]{1,0:T(8,128)(2,1)} %get-tuple-element.241.rows_ref.mine_ref) | copy-start | bytes 2359300 | tf_op jit(solution)/shard_map/cond/branch_1_fun/cond
  9.7 22.3 %collective-permute-start.45 = (bf16[1024,384]{1,0:T(8,128)(2,1)}, bf16[1024,384]{1,0:T(8,128)(2,1)S(1)}, u32[]{:S(2)}, u32[]{:S(2)}) collective-permute-start(bf16[1024,384]{1,0:T(8,128)(2,1)} %get-tuple-element.241.rows_ref.mine_ref), channel_id=1, source_target_pairs={{0,12},{1,13},{2,14},{3,15},{4,8},{5,9},{6,10},{7,11},{8,27},{9,26... | collective-permute-start | bytes 2359304 | tf_op jit(solution)/shard_map/cond/branch_1_fun/cond/branch_4_fun/ppermute | solution.py:33
  13.8 36.8 %collective-permute-start.44 = (bf16[1024,384]{1,0:T(8,128)(2,1)}, bf16[1024,384]{1,0:T(8,128)(2,1)S(1)}, u32[]{:S(2)}, u32[]{:S(2)}) collective-permute-start(bf16[1024,384]{1,0:T(8,128)(2,1)} %get-tuple-element.241.rows_ref.mine_ref), channel_id=1, source_target_pairs={{0,19},{1,18},{2,17},{3,16},{4,23},{5,22},{6,21},{7,20},{8,4},{9,5... | collective-permute-start | bytes 2359304 | tf_op jit(solution)/shard_map/cond/branch_1_fun/cond/branch_4_fun/ppermute | solution.py:33
  32.1 0.9 copy-start.12
  42.7 71.7 %collective-permute-start.47 = (bf16[384,1024]{1,0:T(8,128)(2,1)}, bf16[384,1024]{1,0:T(8,128)(2,1)}, u32[]{:S(2)}, u32[]{:S(2)}) collective-permute-start(bf16[384,1024]{1,0:T(8,128)(2,1)} %get-tuple-element.247), channel_id=1, source_target_pairs={{0,19},{1,18},{2,17},{3,16},{4,23},{5,22},{6,21},{7,20},{8,4},{9,5... | collective-permute-start | bytes 2359304 | tf_op jit(solution)/shard_map/cond/branch_1_fun/cond/branch_4_fun/ppermute | solution.py:33
  50.6 0.9 copy-start.20
  61.2 55.8 %collective-permute-start.46 = (bf16[384,1024]{1,0:T(8,128)(2,1)}, bf16[384,1024]{1,0:T(8,128)(2,1)}, u32[]{:S(2)}, u32[]{:S(2)}) collective-permute-start(bf16[384,1024]{1,0:T(8,128)(2,1)} %get-tuple-element.246), channel_id=1, source_target_pairs={{0,12},{1,13},{2,14},{3,15},{4,8},{5,9},{6,10},{7,11},{8,27},{9,26... | collective-permute-start | bytes 2359304 | tf_op jit(solution)/shard_map/cond/branch_1_fun/cond/branch_4_fun/ppermute | solution.py:33
  119.9 1.8 %collective-permute-start.60 = (f32[256,384]{1,0:T(8,128)S(1)}, f32[256,384]{1,0:T(8,128)S(1)}, u32[]{:S(2)}, u32[]{:S(2)}) collective-permute-start(f32[256,384]{1,0:T(8,128)S(1)} %get-tuple-element.282), channel_id=1, source_target_pairs={{0,1},{1,0},{2,3},{3,2},{4,5},{5,4},{6,7},{7,6},{8,9},{9,8},{10,11... | collective-permute-start | bytes 1179656 | tf_op jit(solution)/shard_map/ppermute | solution.py:21
  121.8 4.2 %collective-permute-start.61 = (bf16[64,384]{1,0:T(8,128)(2,1)S(1)}, bf16[64,384]{1,0:T(8,128)(2,1)S(1)}, u32[]{:S(2)}, u32[]{:S(2)}) collective-permute-start(bf16[64,384]{1,0:T(8,128)(2,1)S(1)} %get-tuple-element.285), channel_id=1, source_target_pairs={{0,2},{1,3},{2,0},{3,1},{4,6},{5,7},{6,4},{7,5},{8,10},{9,11},{10,... | collective-permute-start | bytes 147464 | tf_op jit(solution)/shard_map/ppermute | solution.py:21
  121.8 4.2 %collective-permute-start.62 = (bf16[64,384]{1,0:T(8,128)(2,1)S(1)}, bf16[64,384]{1,0:T(8,128)(2,1)S(1)}, u32[]{:S(2)}, u32[]{:S(2)}) collective-permute-start(bf16[64,384]{1,0:T(8,128)(2,1)S(1)} %get-tuple-element.287), channel_id=1, source_target_pairs={{0,4},{1,5},{2,6},{3,7},{4,0},{5,1},{6,2},{7,3},{8,12},{9,13},{10,... | collective-permute-start | bytes 147464 | tf_op jit(solution)/shard_map/ppermute | solution.py:21
  123.4 5.0 %collective-permute-start.63 = (bf16[64,384]{1,0:T(8,128)(2,1)S(1)}, bf16[64,384]{1,0:T(8,128)(2,1)S(1)}, u32[]{:S(2)}, u32[]{:S(2)}) collective-permute-start(bf16[64,384]{1,0:T(8,128)(2,1)S(1)} %get-tuple-element.286), channel_id=1, source_target_pairs={{0,6},{1,7},{2,4},{3,5},{4,2},{5,3},{6,0},{7,1},{8,14},{9,15},{10,... | collective-permute-start | bytes 147464 | tf_op jit(solution)/shard_map/ppermute | solution.py:21
  128.4 4.5 %collective-permute-start.64 = (f32[16,384]{1,0:T(8,128)S(1)}, f32[16,384]{1,0:T(8,128)S(1)}, u32[]{:S(2)}, u32[]{:S(2)}) collective-permute-start(f32[16,384]{1,0:T(8,128)S(1)} %get-tuple-element.288), channel_id=1, source_target_pairs={{0,8},{1,9},{2,10},{3,11},{4,12},{5,13},{6,14},{7,15},{8,0},{9,1},... | collective-permute-start | bytes 73736 | tf_op jit(solution)/shard_map/ppermute | solution.py:21
  128.5 5.6 %collective-permute-start.65 = (f32[16,384]{1,0:T(8,128)S(1)}, f32[16,384]{1,0:T(8,128)S(1)}, u32[]{:S(2)}, u32[]{:S(2)}) collective-permute-start(f32[16,384]{1,0:T(8,128)S(1)} %get-tuple-element.290), channel_id=1, source_target_pairs={{0,16},{1,17},{2,18},{3,19},{4,20},{5,21},{6,22},{7,23},{8,24},{9,... | collective-permute-start | bytes 73736 | tf_op jit(solution)/shard_map/ppermute | solution.py:21
  132.2 5.6 %collective-permute-start.66 = (f32[16,384]{1,0:T(8,128)S(1)}, f32[16,384]{1,0:T(8,128)S(1)}, u32[]{:S(2)}, u32[]{:S(2)}) collective-permute-start(f32[16,384]{1,0:T(8,128)S(1)} %get-tuple-element.289), channel_id=1, source_target_pairs={{0,24},{1,25},{2,26},{3,27},{4,28},{5,29},{6,30},{7,31},{8,16},{9,... | collective-permute-start | bytes 73736 | tf_op jit(solution)/shard_map/ppermute | solution.py:21
